TPU v7x, 1024 devices: a whole 4x4x32 slice. The times are simulated.
1024 devices in a mesh: gx: 64 (over z, core), gy: 16 (over y, x).
Axes of the slice: x: 4, y: 4, z: 32, core: 2. Of those that a mesh axis runs over, the one named last changes fastest.
Arguments:
- density: float32 [512, 512, 256], P('gx', 'gy'), may hold values from 0.5 to 2
- energy: float32 [512, 512, 256], P('gx', 'gy'), may hold values from 0.5 to 2
- velocity_x: float32 [512, 512, 256], P('gx', 'gy'), may hold values from -0.5 to 0.5
- velocity_y: float32 [512, 512, 256], P('gx', 'gy'), may hold values from -0.5 to 0.5
- velocity_z: float32 [512, 512, 256], P('gx', 'gy'), may hold values from -0.5 to 0.5
- time_step: float32 [1], replicated, may hold values from 0.1 to 0.2
Outputs:
- new_density: float32 [512, 512, 256], P('gx', 'gy')
- new_energy: float32 [512, 512, 256], P('gx', 'gy')
- new_velocity_x: float32 [512, 512, 256], P('gx', 'gy')
- new_velocity_y: float32 [512, 512, 256], P('gx', 'gy')
- new_velocity_z: float32 [512, 512, 256], P('gx', 'gy')
- next_step: float32 [1], replicated
All inputs are finite; a program needn't handle non-finite values.
Results may differ from a plain program's by a relative error of at most 0.0003.
Values sent between devices are 32-bit elements; how exact they have to be, the bound alone decides.
No kernel may reach another device: no remote copies, remote signals or barrier semaphores. Data moves between devices by JAX's collectives and lax.ppermute only.
A program may use at most 32 MiB of HBM per device.

v0:
```python
import functools

import jax
import jax.numpy as jnp
from jax import lax
from jax.sharding import Mesh
from jax.sharding import PartitionSpec as P

GX_GY = ("gx_0", "gx_1", "gy_0", "gy_1")
GX = ("gx_0", "gx_1")
GY = ("gy_0", "gy_1")


def padded_2(block, sides, width):
    for axis, dim in sides:
        count = lax.axis_size(axis)
        forward = [(i, i + 1) for i in range(count - 1)]
        forward.append((count - 1, 0))
        backward = [(target, source) for source, target in forward]
        low = lax.ppermute(
            lax.slice_in_dim(block, block.shape[dim] - width, None, axis=dim), axis, forward
        )
        high = lax.ppermute(lax.slice_in_dim(block, 0, width, axis=dim), axis, backward)
        block = jnp.concatenate([low, block, high], axis=dim)
    return block


def by_axis(x, axes):
    return functools.reduce(lax.pmin, axes, x)


def shifted(field, offset, along):
    return jnp.roll(field, -offset, along)


def van_leer(left_diff, right_diff):
    product = left_diff * right_diff
    agree = product > 0
    return jnp.where(agree, 2.0 * product / jnp.where(agree, left_diff + right_diff, 1.0), 0.0)


def centre(field):
    return field[1:-1, 1:-1]


def diff_x(field):
    return 0.5 * (field[2:, 1:-1] - field[:-2, 1:-1])


def diff_y(field):
    return 0.5 * (field[1:-1, 2:] - field[1:-1, :-2])


def diff_z(field):
    inner = centre(field)
    return 0.5 * (shifted(inner, 1, 2) - shifted(inner, -1, 2))


def lagrange(density, energy, velocity_x, velocity_y, velocity_z, delta_t):
    pressure = 0.4 * density * energy
    diverge = diff_x(velocity_x) + diff_y(velocity_y) + diff_z(velocity_z)
    dens_core = centre(density)
    energy_core = centre(energy)
    press_core = centre(pressure)
    volume = 1.0 + delta_t * diverge
    lag_density = dens_core / volume
    energy_half = energy_core - 0.5 * delta_t * press_core * diverge / dens_core
    press_half = 0.4 * dens_core * energy_half
    lag_energy = energy_core - delta_t * press_half * diverge / dens_core
    new_velx = centre(velocity_x) - delta_t * diff_x(pressure) / dens_core
    new_vely = centre(velocity_y) - delta_t * diff_y(pressure) / dens_core
    new_velz = centre(velocity_z) - delta_t * diff_z(pressure) / dens_core
    return (lag_density, lag_energy, new_velx, new_vely, new_velz)


def sweep_cut(density, mass_energy, velocity, delta_t, along):

    def window(field, lower, upper):
        return lax.slice_in_dim(field, lower, field.shape[along] - upper, axis=along)

    courant = delta_t * (0.5 * (window(velocity, 1, 2) + window(velocity, 2, 1)))
    weight = 0.5 * (1.0 - jnp.abs(courant))

    def face_value(field):
        slope = van_leer(
            window(field, 1, 1) - window(field, 0, 2), window(field, 2, 0) - window(field, 1, 1)
        )
        ahead = window(field, 1, 2) + weight * window(slope, 0, 1)
        behind = window(field, 2, 1) - weight * window(slope, 1, 0)
        return jnp.where(courant > 0, ahead, behind)

    flux = courant * face_value(density)
    energy_flux = courant * face_value(mass_energy)
    dens_out = window(density, 2, 2) + window(flux, 0, 1) - window(flux, 1, 0)
    mass_out = window(mass_energy, 2, 2) + window(energy_flux, 0, 1) - window(energy_flux, 1, 0)
    return (dens_out, mass_out)


def sweep_roll(density, mass_energy, velocity, delta_t, along):
    courant = delta_t * (0.5 * (velocity + shifted(velocity, 1, along)))
    weight = 0.5 * (1.0 - jnp.abs(courant))

    def face_value(field):
        slope = van_leer(field - shifted(field, -1, along), shifted(field, 1, along) - field)
        ahead = field + weight * slope
        behind = shifted(field, 1, along) - weight * shifted(slope, 1, along)
        return jnp.where(courant > 0, ahead, behind)

    flux = courant * face_value(density)
    energy_flux = courant * face_value(mass_energy)
    dens_out = density + shifted(flux, -1, along) - flux
    mass_out = mass_energy + shifted(energy_flux, -1, along) - energy_flux
    return (dens_out, mass_out)


def local(density, energy, velocity_x, velocity_y, velocity_z, time_step):
    delta_t = time_step[0]
    stacked = jnp.stack([density, energy, velocity_x, velocity_y, velocity_z])
    padded = padded_2(stacked, ((GX, 1), (GY, 2)), 3)
    lag_density, lag_energy, wide_velx, wide_vely, wide_velz = lagrange(
        padded[0], padded[1], padded[2], padded[3], padded[4], delta_t
    )
    mass_energy = lag_density * lag_energy
    dens_a, mass_a = sweep_cut(lag_density, mass_energy, wide_velx, delta_t, 0)
    dens_b, mass_b = sweep_cut(dens_a, mass_a, wide_vely[2:-2], delta_t, 1)
    new_velx = wide_velx[2:-2, 2:-2]
    new_vely = wide_vely[2:-2, 2:-2]
    new_velz = wide_velz[2:-2, 2:-2]
    dens_c, mass_c = sweep_roll(dens_b, mass_b, new_velz, delta_t, 2)
    new_energy = mass_c / dens_c
    speed = jnp.sqrt(0.56 * new_energy) + jnp.abs(new_velx) + jnp.abs(new_vely) + jnp.abs(new_velz)
    limit = by_axis(jnp.min(0.5 / speed), GX_GY)
    return (dens_c, new_energy, new_velx, new_vely, new_velz, limit.reshape(1))


def solution(mesh):
    finer = Mesh(mesh.devices.reshape(32, 2, 4, 4), ("gx_0", "gx_1", "gy_0", "gy_1"))
    in_specs = (
        P(GX, GY, None),
        P(GX, GY, None),
        P(GX, GY, None),
        P(GX, GY, None),
        P(GX, GY, None),
        P(),
    )
    out_specs = (
        P(GX, GY, None),
        P(GX, GY, None),
        P(GX, GY, None),
        P(GX, GY, None),
        P(GX, GY, None),
        P(),
    )
    return jax.shard_map(local, mesh=finer, in_specs=in_specs, out_specs=out_specs, check_vma=False)
```

profile of v0, /device:TPU:10, one launch (start us, length us, event | category | flops | bytes accessed | tf_op | source)
XLA Modules:
  0.0 134.2 jit_solution(18397060752442650883)
XLA Ops:
  0.7 1.0 bitcast_dynamic-update-slice_fusion.4
  1.7 1.0 bitcast_dynamic-update-slice_fusion.3
  2.7 1.0 bitcast_dynamic-update-slice_fusion.2
  3.8 16.2 %collective-permute-start.1 = (f32[5,3,32,256]{3,2,1,0:T(8,128)S(1)}, f32[5,3,32,256]{3,2,1,0:T(8,128)S(1)}, u32[]{:S(2)}, u32[]{:S(2)}) collective-permute-start(f32[5,3,32,256]{3,2,1,0:T(8,128)S(1)} %get-tuple-element.24), channel_id=1, source_target_pairs={{16,0},{32,16},{48,32},{64,48},{80,64},{96,80},{112,96},{128,112},... | collective-permute-start | bytes 1474568 | tf_op jit(solution)/shard_map/ppermute | solution.py:23
  20.0 6.3 %collective-permute-done.1 = f32[5,3,32,256]{3,2,1,0:T(8,128)S(1)} collective-permute-done((f32[5,3,32,256]{3,2,1,0:T(8,128)S(1)}, f32[5,3,32,256]{3,2,1,0:T(8,128)S(1)}, u32[]{:S(2)}, u32[]{:S(2)}) %collective-permute-start.1) | collective-permute-done | bytes 491552 | tf_op jit(solution)/shard_map/ppermute | solution.py:23
  26.4 3.1 %collective-permute-done = f32[5,3,32,256]{3,2,1,0:T(8,128)S(1)} collective-permute-done((f32[5,3,32,256]{3,2,1,0:T(8,128)S(1)}, f32[5,3,32,256]{3,2,1,0:T(8,128)S(1)}, u32[]{:S(2)}, u32[]{:S(2)}) %collective-permute-start) | collective-permute-done | bytes 491552 | tf_op jit(solution)/shard_map/ppermute | solution.py:20
  29.6 2.4 %collective-permute-start.3 = (f32[5,14,3,256]{3,2,1,0:T(4,128)S(1)}, f32[5,14,3,256]{3,2,1,0:T(4,128)S(1)}, u32[]{:S(2)}, u32[]{:S(2)}) collective-permute-start(f32[5,14,3,256]{3,2,1,0:T(4,128)S(1)} %get-tuple-element.21), channel_id=1, source_target_pairs={{1,0},{2,1},{3,2},{4,3},{5,4},{6,5},{7,6},{8,7},{9,8},{10,9},{11,1... | collective-permute-start | bytes 645128 | tf_op jit(solution)/shard_map/ppermute | solution.py:23
  32.0 3.4 %collective-permute-start.2 = (f32[5,14,3,256]{3,2,1,0:T(4,128)S(1)}, f32[5,14,3,256]{3,2,1,0:T(4,128)S(1)}, u32[]{:S(2)}, u32[]{:S(2)}) collective-permute-start(f32[5,14,3,256]{3,2,1,0:T(4,128)S(1)} %get-tuple-element.20), channel_id=1, source_target_pairs={{0,1},{1,2},{2,3},{3,4},{4,5},{5,6},{6,7},{7,8},{8,9},{9,10},{10,1... | collective-permute-start | bytes 645128 | tf_op jit(solution)/shard_map/ppermute | solution.py:20
  36.1 2.0 %collective-permute-done.3 = f32[5,14,3,256]{3,2,1,0:T(4,128)S(1)} collective-permute-done((f32[5,14,3,256]{3,2,1,0:T(4,128)S(1)}, f32[5,14,3,256]{3,2,1,0:T(4,128)S(1)}, u32[]{:S(2)}, u32[]{:S(2)}) %collective-permute-start.3) | collective-permute-done | bytes 215072 | tf_op jit(solution)/shard_map/ppermute | solution.py:23
  38.1 3.1 %collective-permute-done.2 = f32[5,14,3,256]{3,2,1,0:T(4,128)S(1)} collective-permute-done((f32[5,14,3,256]{3,2,1,0:T(4,128)S(1)}, f32[5,14,3,256]{3,2,1,0:T(4,128)S(1)}, u32[]{:S(2)}, u32[]{:S(2)}) %collective-permute-start.2) | collective-permute-done | bytes 215072 | tf_op jit(solution)/shard_map/ppermute | solution.py:20
  41.2 0.5 pad_maximum_fusion
  41.8 0.2 slice_bitcast_fusion.3
  42.0 0.2 fusion.54
  42.4 0.2 fusion.53
  42.7 0.8 fusion.18
  43.5 0.5 add_divide_fusion
  44.3 0.2 fusion.25
  44.6 0.2 divide_select_fusion.3
  44.8 0.2 divide_select_fusion.2
  44.9 0.4 fusion.34
  45.6 0.2 divide_select_fusion.4
  46.2 0.3 copy-done
  46.8 0.2 divide_select_fusion.5
  47.1 0.5 copy-done.1
  47.6 0.2 fusion.44
  48.0 0.2 fusion.40
  48.3 0.3 copy-done.2
  48.6 1.9 %fusion.47 = (f32[]{:T(128)}, f32[8,32,256]{2,1,0:T(8,128)}, f32[8,32,256]{2,1,0:T(8,128)}, f32[8,32,256]{2,1,0:T(8,128)}, f32[8,32,256]{2,1,0:T(8,128)}) fusion(f32[8,32,256]{2,1,0:T(8,128)S(1)} %get-tuple-element.12, f32[12,36,256]{2,1,0:T(8,128)S(1)} %get-tuple-element.22, f32[12,36,256]{2,1,0:T(8,128)S(1)} %get-tuple-element.27, ...), kind=kLoop, calls=%fused_computation.116 | loop fusion | flops 1048575 | bytes 3407876 | tf_op jit(solution)/shard_map/reduce_min | solution.py:132
  50.5 55.9 %pmin.28 = f32[]{:T(128)} all-reduce(f32[]{:T(128)} %get-tuple-element.6), channel_id=1, replica_groups=mesh['gx_0'=32,'gx_1'=2,'gy_0'=4,'gy_1'=4] {'gx_0'}, use_global_device_ids=true, to_apply=%region_1.2 | all-reduce | flops 1 | bytes 8 | tf_op jit(solution)/shard_map/pmin | solution.py:29
  106.4 3.1 %pmin.29 = f32[]{:T(128)} all-reduce(f32[]{:T(128)} %pmin.28), channel_id=1, replica_groups=mesh['gx_0'=32,'gx_1'=2,'gy_0'=4,'gy_1'=4] {'gx_1'}, use_global_device_ids=true, to_apply=%region_2.3 | all-reduce | flops 1 | bytes 8 | tf_op jit(solution)/shard_map/pmin | solution.py:29
  109.5 11.3 %pmin.30 = f32[]{:T(128)} all-reduce(f32[]{:T(128)} %pmin.29), channel_id=1, replica_groups=mesh['gx_0'=32,'gx_1'=2,'gy_0'=4,'gy_1'=4] {'gy_0'}, use_global_device_ids=true, to_apply=%region_3.4 | all-reduce | flops 1 | bytes 8 | tf_op jit(solution)/shard_map/pmin | solution.py:29
  120.8 13.3 %pmin.31 = f32[1]{0:T(128)} all-reduce(f32[1]{0:T(128)} %bitcast.11), channel_id=1, replica_groups=mesh['gx_0'=32,'gx_1'=2,'gy_0'=4,'gy_1'=4] {'gy_1'}, use_global_device_ids=true, to_apply=%region_4.5 | all-reduce | flops 1 | bytes 8 | tf_op jit(solution)/shard_map/pmin | solution.py:29
  (33 shorter events, 2.1 us)
Async XLA Ops:
  0.6 3.0 %copy-start.3 = (f32[8,32,256]{2,1,0:T(8,128)S(1)}, f32[8,32,256]{2,1,0:T(8,128)}, u32[]{:S(2)}) copy-start(f32[8,32,256]{2,1,0:T(8,128)} %param.9) | copy-start | bytes 786436
  0.6 3.0 %copy-start.4 = (f32[8,32,256]{2,1,0:T(8,128)S(1)}, f32[8,32,256]{2,1,0:T(8,128)}, u32[]{:S(2)}) copy-start(f32[8,32,256]{2,1,0:T(8,128)} %param.10) | copy-start | bytes 786436
  3.8 22.6 %collective-permute-start.1 = (f32[5,3,32,256]{3,2,1,0:T(8,128)S(1)}, f32[5,3,32,256]{3,2,1,0:T(8,128)S(1)}, u32[]{:S(2)}, u32[]{:S(2)}) collective-permute-start(f32[5,3,32,256]{3,2,1,0:T(8,128)S(1)} %get-tuple-element.24), channel_id=1, source_target_pairs={{16,0},{32,16},{48,32},{64,48},{80,64},{96,80},{112,96},{128,112},... | collective-permute-start | bytes 1474568 | tf_op jit(solution)/shard_map/ppermute | solution.py:23
  20.0 9.5 %collective-permute-start = (f32[5,3,32,256]{3,2,1,0:T(8,128)S(1)}, f32[5,3,32,256]{3,2,1,0:T(8,128)S(1)}, u32[]{:S(2)}, u32[]{:S(2)}) collective-permute-start(f32[5,3,32,256]{3,2,1,0:T(8,128)S(1)} %get-tuple-element.23), channel_id=1, source_target_pairs={{0,16},{16,32},{32,48},{48,64},{64,80},{80,96},{96,112},{112,128},... | collective-permute-start | bytes 1474568 | tf_op jit(solution)/shard_map/ppermute | solution.py:20
  29.6 8.5 %collective-permute-start.3 = (f32[5,14,3,256]{3,2,1,0:T(4,128)S(1)}, f32[5,14,3,256]{3,2,1,0:T(4,128)S(1)}, u32[]{:S(2)}, u32[]{:S(2)}) collective-permute-start(f32[5,14,3,256]{3,2,1,0:T(4,128)S(1)} %get-tuple-element.21), channel_id=1, source_target_pairs={{1,0},{2,1},{3,2},{4,3},{5,4},{6,5},{7,6},{8,7},{9,8},{10,9},{11,1... | collective-permute-start | bytes 645128 | tf_op jit(solution)/shard_map/ppermute | solution.py:23
  32.0 9.2 %collective-permute-start.2 = (f32[5,14,3,256]{3,2,1,0:T(4,128)S(1)}, f32[5,14,3,256]{3,2,1,0:T(4,128)S(1)}, u32[]{:S(2)}, u32[]{:S(2)}) collective-permute-start(f32[5,14,3,256]{3,2,1,0:T(4,128)S(1)} %get-tuple-element.20), channel_id=1, source_target_pairs={{0,1},{1,2},{2,3},{3,4},{4,5},{5,6},{6,7},{7,8},{8,9},{9,10},{10,1... | collective-permute-start | bytes 645128 | tf_op jit(solution)/shard_map/ppermute | solution.py:20
  45.8 0.7 copy-start
  46.7 1.0 copy-start.1
  46.7 1.0 slice-start
  47.9 0.7 copy-start.2
where the time goes:
time: 135 us; the launch traced here: 134 us
  blocking collectives  83.7 us (62%)
  starting transfers between devices  22.1 us (16%)
  waiting for transfers between devices  14.6 us (11%)
  local copies, waits for them, and re-layouts  6.15 us (5%)
  other arithmetic  6.08 us (5%)
  between operations  1.64 us (1%)
    pmin x4, blocking collectives, by_axis(): return functools.reduce(lax.pmin, axes, x)  83.7 us
    ppermute x2, starting transfers between devices, padded_2(): lax.ppermute(lax.slice_in_dim(block, 0, width, axis=dim), axis, backward)  18.7 us
    ppermute x2, waiting for transfers between devices, padded_2(): lax.ppermute(lax.slice_in_dim(block, 0, width, axis=dim), axis, backward)  8.37 us
    ppermute x2, waiting for transfers between devices, padded_2(): lax.ppermute(lax.slice_in_dim(block, block.shape[dim] - width, None, axis...  6.2 us
    unnamed x14, local copies, waits for them, and re-layouts  4.08 us
    ppermute x2, starting transfers between devices, padded_2(): lax.ppermute(lax.slice_in_dim(block, block.shape[dim] - width, None, axis...  3.4 us
  transfers between devices with their start and end apart: 4, of which 4 were waited for; matrix products, arithmetic and copies ran while one was open for 0% of the time, Pallas kernels for 0%

commit v1 on v0

v1 whole, which is shorter than its diff:
```python
import jax
import jax.numpy as jnp
from jax import lax
from jax.experimental import pallas as pl
from jax.experimental.pallas import tpu as pltpu
from jax.sharding import Mesh
from jax.sharding import PartitionSpec as P

AXES = ("z", "c", "y", "x")
GX = ("z", "c")
GY = ("y", "x")
PLANE = ("c", "y", "x")

X_WIDTH = (3, 2, 2, 2, 2)
X_BASE = (0, 3, 5, 7, 9)
X_ROWS = 11
Y_WIDTH = (2, 3, 2, 2, 2)
Y_PLANES = (14, 12, 12, 12, 12)
Y_BASE = (0, 28, 64, 88, 112)
Y_ROWS = 136
PAD = 40


def plane_of(field, index, own, low, high):
    width, base = X_WIDTH[field], X_BASE[field]
    if index < 0:
        return low.at[base + index + width]
    if index >= 8:
        return high.at[base + index - 8]
    return own[field].at[index]


def pack_y_kernel(vx, vy, vz, den, ene, low, high, up, down):
    own = (vx, vy, vz, den, ene)
    for field in range(5):
        width, reach = Y_WIDTH[field], X_WIDTH[field]
        for k in range(Y_PLANES[field]):
            plane = plane_of(field, k - reach, own, low, high)
            line = Y_BASE[field] + k * width
            up[line : line + width, :] = plane[32 - width : 32, :]
            down[line : line + width, :] = plane[0:width, :]


def above(x, axis):
    return pltpu.roll(x, x.shape[axis] - 1, axis)


def below(x, axis):
    return pltpu.roll(x, 1, axis)


def van_leer(left, right):
    product = left * right
    agree = product > 0
    return jnp.where(agree, 2.0 * product / jnp.where(agree, left + right, 1.0), 0.0)


def sweep_roll(density, mass, velocity, half_t, axis):
    courant = half_t * (velocity + above(velocity, axis))
    weight = 0.5 * (1.0 - jnp.abs(courant))
    forward = courant > 0

    def moved(field):
        ahead = above(field, axis)
        diff = ahead - field
        slope = van_leer(below(diff, axis), diff)
        face = jnp.where(forward, field + weight * slope, ahead - weight * above(slope, axis))
        flux = courant * face
        return field + below(flux, axis) - flux

    return moved(density), moved(mass)


def step_kernel(
    ts, vx, vy, vz, den, ene, xlo, xhi, ylo, yhi,
    o_den, o_ene, o_vx, o_vy, o_vz, o_lim,
    s_vx, s_vy, s_vz, s_d, s_e, s_ld, s_me, s_pr, s_nvx, s_sd, s_sm, s_fd, s_fm, s_max,
):
    t = ts[0]
    half_t = 0.5 * t
    own = (vx, vy, vz, den, ene)
    padded = (s_vx, s_vy, s_vz, s_d, s_e)
    for field in range(5):
        width, reach = Y_WIDTH[field], X_WIDTH[field]
        for k in range(Y_PLANES[field]):
            padded[field][k, 0:32, :] = plane_of(field, k - reach, own, xlo, xhi)[...]
            line = Y_BASE[field] + k * width
            padded[field][k, 32 : 32 + width, :] = yhi[line : line + width, :]
            padded[field][k, 40 - width : 40, :] = ylo[line : line + width, :]

    def lagrange(i, carry):
        rho, en = s_d[i], s_e[i]
        v = s_vy[i]
        w = s_vz[i]
        diverge = 0.5 * (s_vx[i + 2] - s_vx[i])
        diverge = diverge + 0.5 * (above(v, 0) - below(v, 0))
        diverge = diverge + 0.5 * (above(w, 1) - below(w, 1))
        move = t * diverge
        lag_density = rho / (1.0 + move)
        energy_half = en - 0.2 * en * move
        lag_energy = en - 0.4 * energy_half * move
        s_ld[i] = lag_density
        s_me[i] = lag_density * lag_energy
        s_pr[i] = 0.4 * rho * en
        return carry

    lax.fori_loop(0, 12, lagrange, 0)

    def velocity_x(i, carry):
        s_nvx[i] = s_vx[i + 2] - half_t * (s_pr[i + 2] - s_pr[i]) / s_d[i + 1]
        s_sd[i] = van_leer(s_ld[i + 1] - s_ld[i], s_ld[i + 2] - s_ld[i + 1])
        s_sm[i] = van_leer(s_me[i + 1] - s_me[i], s_me[i + 2] - s_me[i + 1])
        return carry

    lax.fori_loop(0, 10, velocity_x, 0)

    def flux_x(i, carry):
        courant = half_t * (s_nvx[i] + s_nvx[i + 1])
        weight = 0.5 * (1.0 - jnp.abs(courant))
        forward = courant > 0
        s_fd[i] = courant * jnp.where(forward, s_ld[i + 1] + weight * s_sd[i], s_ld[i + 2] - weight * s_sd[i + 1])
        s_fm[i] = courant * jnp.where(forward, s_me[i + 1] + weight * s_sm[i], s_me[i + 2] - weight * s_sm[i + 1])
        return carry

    lax.fori_loop(0, 9, flux_x, 0)

    s_max[...] = jnp.zeros_like(s_max)

    def finish(p, carry):
        pressure = s_pr[p + 2]
        over = half_t / s_d[p + 2]
        new_vy = s_vy[p + 2] - over * (above(pressure, 0) - below(pressure, 0))
        dens = s_ld[p + 2] + s_fd[p] - s_fd[p + 1]
        mass = s_me[p + 2] + s_fm[p] - s_fm[p + 1]
        dens, mass = sweep_roll(dens, mass, new_vy, half_t, 0)
        dens, mass, new_vy = dens[:32], mass[:32], new_vy[:32]
        pressure, over = pressure[:32], over[:32]
        new_vz = s_vz[p + 2, 0:32, :] - over * (above(pressure, 1) - below(pressure, 1))
        dens, mass = sweep_roll(dens, mass, new_vz, half_t, 1)
        energy = mass / dens
        new_vx = s_nvx[p + 1, 0:32, :]
        speed = jnp.sqrt(0.56 * energy) + jnp.abs(new_vx) + jnp.abs(new_vy) + jnp.abs(new_vz)
        o_den[p] = dens
        o_ene[p] = energy
        o_vx[p] = new_vx
        o_vy[p] = new_vy
        o_vz[p] = new_vz
        s_max[...] = jnp.maximum(s_max[...], speed)
        return carry

    lax.fori_loop(0, 8, finish, 0)
    fastest = jnp.max(s_max[...], axis=0, keepdims=True)
    fastest = jnp.maximum(fastest[:, :128], fastest[:, 128:])
    o_lim[...] = jnp.broadcast_to(0.5 / fastest, o_lim.shape)


def shift(x, axes, count, by):
    return lax.ppermute(x, axes, [(i, (i + by) % count) for i in range(count)])


def smallest(spread, sizes):
    nz, count = sizes["z"], spread.shape[0]
    part = jnp.min(lax.all_to_all(spread, PLANE, 0, 0, tiled=True), axis=0, keepdims=True)
    pairs = [(z * count + k, ((z + k) % nz) * count + k) for z in range(nz) for k in range(count)]
    part = lax.ppermute(part, AXES, pairs)
    part = lax.all_to_all(jnp.broadcast_to(part, spread.shape), PLANE, 0, 0, tiled=True)
    return jnp.min(part).reshape(1)


def solution(mesh):
    gx, gy = mesh.devices.shape
    sizes = {"z": gx // 2, "c": 2, "y": 4 if gy == 16 else 1, "x": gy // (4 if gy == 16 else 1)}
    finer = Mesh(mesh.devices.reshape(tuple(sizes[a] for a in AXES)), AXES)
    plane = sizes["c"] * sizes["y"] * sizes["x"]
    assert plane == sizes["z"]
    vmem = pl.BlockSpec(memory_space=pltpu.VMEM)
    tile = jax.ShapeDtypeStruct((8, 32, 256), jnp.float32)
    lines = jax.ShapeDtypeStruct((Y_ROWS, 256), jnp.float32)
    pack_y = pl.pallas_call(
        pack_y_kernel,
        out_shape=(lines, lines),
        in_specs=[vmem] * 7,
        out_specs=(vmem, vmem),
        name="pack_y",
    )
    step = pl.pallas_call(
        step_kernel,
        out_shape=(tile,) * 5 + (jax.ShapeDtypeStruct((plane, 128), jnp.float32),),
        in_specs=[pl.BlockSpec(memory_space=pltpu.SMEM)] + [vmem] * 9,
        out_specs=(vmem,) * 6,
        scratch_shapes=[pltpu.VMEM((n, PAD, 256), jnp.float32) for n in (14, 12, 12, 12, 12, 12, 12, 12, 10, 10, 10, 9, 9)]
        + [pltpu.VMEM((32, 256), jnp.float32)],
        name="remap",
    )

    def local(density, energy, velocity_x, velocity_y, velocity_z, time_step):
        fields = (velocity_x, velocity_y, velocity_z, density, energy)
        first = jnp.concatenate([f[:w] for f, w in zip(fields, X_WIDTH)], axis=0)
        last = jnp.concatenate([f[8 - w :] for f, w in zip(fields, X_WIDTH)], axis=0)
        xlo = shift(last, GX, gx, 1)
        xhi = shift(first, GX, gx, -1)
        up, down = pack_y(*fields, xlo, xhi)
        ylo = shift(up, GY, gy, 1)
        yhi = shift(down, GY, gy, -1)
        *outs, spread = step(time_step, *fields, xlo, xhi, ylo, yhi)
        return (*outs, smallest(spread, sizes))

    split = P(GX, GY, None)
    return jax.shard_map(
        local, mesh=finer, in_specs=(split,) * 5 + (P(),), out_specs=(split,) * 5 + (P(),), check_vma=False
    )
```

time: 135 us -> 101 us (0.75)
  the two profiles are of different devices: /device:TPU:10 before, /device:TPU:1 now
where the time goes in v1:
time: 101 us
  starting transfers between devices  35.4 us (35%)
  blocking collectives  32.8 us (32%)
  waiting for transfers between devices  16.5 us (16%)
  Pallas kernels  10.4 us (10%)
  local copies, waits for them, and re-layouts  3.47 us (3%)
  between operations  1.37 us (1%)
    ppermute x4, starting transfers between devices, shift(): return lax.ppermute(x, axes, [(i, (i + by) % count) for i in range(count)])  22.9 us
    all_to_all x1, blocking collectives, smallest(): lax.all_to_all(spread, PLANE, 0, 0, tiled=True)  21.9 us
    ppermute x1, starting transfers between devices, smallest(): part = lax.ppermute(part, AXES, pairs)  12.5 us
    all_to_all x1, blocking collectives, smallest(): lax.all_to_all(jnp.broadcast_to(part, spread.shape), PLANE, 0, 0, tiled=T...  10.9 us
    ppermute x1, waiting for transfers between devices, smallest(): part = lax.ppermute(part, AXES, pairs)  10.1 us
    pallas_call x1, Pallas kernels, local(): *outs, spread = step(time_step, *fields, xlo, xhi, ylo, yhi)  8.14 us
    ppermute x4, waiting for transfers between devices, shift(): return lax.ppermute(x, axes, [(i, (i + by) % count) for i in range(count)])  6.42 us
    unnamed x20, local copies, waits for them, and re-layouts  3.45 us
  transfers between devices with their start and end apart: 5, of which 5 were waited for; matrix products, arithmetic and copies ran while one was open for 0% of the time, Pallas kernels for 0%

profile of v1, /device:TPU:1, one launch (start us, length us, event | category | flops | bytes accessed | tf_op | source)
XLA Modules:
  0.0 100.6 jit_solution(15105098908817455768)
XLA Ops:
  0.6 0.0 copy-start
  0.6 0.0 copy-start.1
  0.7 1.0 %slice_dynamic-update-slice_fusion = (f32[11,32,256]{2,1,0:T(8,128)S(1)}, f32[11,32,256]{2,1,0:T(8,128)S(1)}) fusion(f32[8,32,256]{2,1,0:T(8,128)} %vx.3), kind=kLoop, calls=%fused_computation | loop fusion | bytes 393216
  1.7 0.0 copy-done
  1.7 0.0 copy-start.2
  1.7 0.0 copy-done.1
  1.8 0.0 copy-start.3
  1.8 0.9 copy-done.2
  2.7 0.1 copy-done.3
  2.7 14.1 %collective-permute-start.1 = (f32[11,32,256]{2,1,0:T(8,128)S(1)}, f32[11,32,256]{2,1,0:T(8,128)S(1)}, u32[]{:S(2)}, u32[]{:S(2)}) collective-permute-start(f32[11,32,256]{2,1,0:T(8,128)S(1)} %get-tuple-element.22), channel_id=1, source_target_pairs={{0,1008},{16,0},{32,16},{48,32},{64,48},{80,64},{96,80},{112,96},{... | collective-permute-start | bytes 1081352 | tf_op jit(solution)/shard_map/ppermute | solution.py:158
  16.9 0.0 collective-permute-start
  16.9 1.3 %collective-permute-done.1.high.xhi = f32[11,32,256]{2,1,0:T(8,128)S(1)} collective-permute-done((f32[11,32,256]{2,1,0:T(8,128)S(1)}, f32[11,32,256]{2,1,0:T(8,128)S(1)}, u32[]{:S(2)}, u32[]{:S(2)}) %collective-permute-start.1) | collective-permute-done | bytes 360480 | tf_op jit(solution)/shard_map/ppermute | solution.py:158
  18.2 0.0 copy-start.4
  18.2 3.5 %collective-permute-done.low.xlo = f32[11,32,256]{2,1,0:T(8,128)S(1)} collective-permute-done((f32[11,32,256]{2,1,0:T(8,128)S(1)}, f32[11,32,256]{2,1,0:T(8,128)S(1)}, u32[]{:S(2)}, u32[]{:S(2)}) %collective-permute-start) | collective-permute-done | bytes 360480 | tf_op jit(solution)/shard_map/ppermute | solution.py:158
  21.6 0.0 copy-done.4
  21.6 0.0 copy-start.5
  21.6 0.7 copy-done.5
  22.4 2.3 %pack_y.1 = (f32[136,256]{1,0:T(8,128)}, f32[136,256]{1,0:T(8,128)}) custom-call(f32[8,32,256]{2,1,0:T(8,128)} %vx.3, f32[8,32,256]{2,1,0:T(8,128)} %vy.3, f32[8,32,256]{2,1,0:T(8,128)} %vz.3, f32[8,32,256]{2,1,0:T(8,128)} %den.3, f32[8,32,256]{2,1,0:T(8,128)} %ene.3, f32[11,32,256]{2,1,0:T(8,128)} %copy-done.5, f32[11,32,256]{2,1,0:T(8,128)} %copy-done.4), custom_call_target="tpu_custom_call" | custom-call | tf_op jit(solution)/shard_map/pack_y/pallas_call | solution.py:202
  24.7 3.1 %collective-permute-start.2 = (f32[136,256]{1,0:T(8,128)}, f32[136,256]{1,0:T(8,128)S(1)}, u32[]{:S(2)}, u32[]{:S(2)}) collective-permute-start(f32[136,256]{1,0:T(8,128)} %get-tuple-element.14), channel_id=1, source_target_pairs={{0,1},{1,2},{2,3},{3,4},{4,5},{5,6},{6,7},{7,8},{8,9},{9,10},{10,1... | collective-permute-start | bytes 417800 | tf_op jit(solution)/shard_map/ppermute | solution.py:158
  27.8 5.6 %collective-permute-start.3 = (f32[136,256]{1,0:T(8,128)}, f32[136,256]{1,0:T(8,128)S(1)}, u32[]{:S(2)}, u32[]{:S(2)}) collective-permute-start(f32[136,256]{1,0:T(8,128)} %get-tuple-element.15), channel_id=1, source_target_pairs={{0,15},{1,0},{2,1},{3,2},{4,3},{5,4},{6,5},{7,6},{8,7},{9,8},{10,9... | collective-permute-start | bytes 417800 | tf_op jit(solution)/shard_map/ppermute | solution.py:158
  34.1 0.1 collective-permute-done.2.ylo
  34.1 0.0 copy-start.6
  34.1 1.6 %collective-permute-done.3.yhi = f32[136,256]{1,0:T(8,128)S(1)} collective-permute-done((f32[136,256]{1,0:T(8,128)}, f32[136,256]{1,0:T(8,128)S(1)}, u32[]{:S(2)}, u32[]{:S(2)}) %collective-permute-start.3) | collective-permute-done | bytes 139296 | tf_op jit(solution)/shard_map/ppermute | solution.py:158
  35.7 0.0 copy-done.6
  35.7 0.7 copy-done.7
  36.4 8.1 %remap.1 = (f32[8,32,256]{2,1,0:T(8,128)}, f32[8,32,256]{2,1,0:T(8,128)}, f32[8,32,256]{2,1,0:T(8,128)}, f32[8,32,256]{2,1,0:T(8,128)}, f32[8,32,256]{2,1,0:T(8,128)}, /*index=5*/f32[32,128]{1,0:T(8,128)}) custom-call(f32[1]{0:T(128)S(6)} %copy.24.ts, f32[8,32,256]{2,1,0:T(8,128)} %vx.3, f32[8,32,256]{2,1,0:T(8,128)} %vy.3, f32[8,32,256]{2,1,0:T(8,128)} %vz.3, ...), custom_call_target="tpu_custom_call" | custom-call | tf_op jit(solution)/shard_map/remap/pallas_call | solution.py:205
  44.6 21.9 %all_to_all.15 = f32[32,1,128]{2,1,0:T(1,128)S(1)} all-to-all(f32[32,1,128]{2,1,0:T(1,128)} %bitcast.8), channel_id=1, replica_groups=mesh['z'=32,'c'=2,'y'=4,'x'=4] {'c','y','x'}, dimensions={0} | all-to-all | bytes 32768 | tf_op jit(solution)/shard_map/all_to_all | solution.py:163
  66.4 0.1 reduce_min.18
  66.5 12.5 %collective-permute-start.4 = (f32[1,128]{1,0:T(1,128)S(1)}, f32[1,128]{1,0:T(1,128)S(1)}, u32[]{:S(2)}, u32[]{:S(2)}) collective-permute-start(f32[1,128]{1,0:T(1,128)S(1)} %bitcast.9), channel_id=1, source_target_pairs={{0,0},{1,33},{2,66},{3,99},{4,132},{5,165},{6,198},{7,231},{8,264}... | collective-permute-start | bytes 1544 | tf_op jit(solution)/shard_map/ppermute | solution.py:165
  79.0 10.1 %collective-permute-done.4 = f32[1,128]{1,0:T(1,128)S(1)} collective-permute-done((f32[1,128]{1,0:T(1,128)S(1)}, f32[1,128]{1,0:T(1,128)S(1)}, u32[]{:S(2)}, u32[]{:S(2)}) %collective-permute-start.4) | collective-permute-done | bytes 544 | tf_op jit(solution)/shard_map/ppermute | solution.py:165
  89.1 10.9 %all_to_all.16 = f32[32,1,128]{2,1,0:T(1,128)S(1)} all-to-all(f32[32,1,128]{2,1,0:T(1,128)S(1)} %broadcast_in_dim.9), channel_id=1, replica_groups=mesh['z'=32,'c'=2,'y'=4,'x'=4] {'c','y','x'}, dimensions={0} | all-to-all | bytes 32768 | tf_op jit(solution)/shard_map/all_to_all | solution.py:166
  100.0 0.6 reduce_min.19
  (6 shorter events, 0.1 us)
Async XLA Ops:
  0.6 1.0 %copy-start = (f32[8,32,256]{2,1,0:T(8,128)S(1)}, f32[8,32,256]{2,1,0:T(8,128)}, u32[]{:S(2)}) copy-start(f32[8,32,256]{2,1,0:T(8,128)} %vy.3) | copy-start | bytes 786436
  0.6 1.1 %copy-start.1 = (f32[8,32,256]{2,1,0:T(8,128)S(1)}, f32[8,32,256]{2,1,0:T(8,128)}, u32[]{:S(2)}) copy-start(f32[8,32,256]{2,1,0:T(8,128)} %vz.3) | copy-start | bytes 786436
  1.7 1.0 copy-start.2
  1.8 1.0 copy-start.3
  2.7 15.4 %collective-permute-start.1 = (f32[11,32,256]{2,1,0:T(8,128)S(1)}, f32[11,32,256]{2,1,0:T(8,128)S(1)}, u32[]{:S(2)}, u32[]{:S(2)}) collective-permute-start(f32[11,32,256]{2,1,0:T(8,128)S(1)} %get-tuple-element.22), channel_id=1, source_target_pairs={{0,1008},{16,0},{32,16},{48,32},{64,48},{80,64},{96,80},{112,96},{... | collective-permute-start | bytes 1081352 | tf_op jit(solution)/shard_map/ppermute | solution.py:158
  16.9 4.8 %collective-permute-start = (f32[11,32,256]{2,1,0:T(8,128)S(1)}, f32[11,32,256]{2,1,0:T(8,128)S(1)}, u32[]{:S(2)}, u32[]{:S(2)}) collective-permute-start(f32[11,32,256]{2,1,0:T(8,128)S(1)} %get-tuple-element.23), channel_id=1, source_target_pairs={{0,16},{16,32},{32,48},{48,64},{64,80},{80,96},{96,112},{112,128},... | collective-permute-start | bytes 1081352 | tf_op jit(solution)/shard_map/ppermute | solution.py:158
  18.2 3.5 %copy-start.4 = (f32[11,32,256]{2,1,0:T(8,128)}, f32[11,32,256]{2,1,0:T(8,128)S(1)}, u32[]{:S(2)}) copy-start(f32[11,32,256]{2,1,0:T(8,128)S(1)} %collective-permute-done.1.high.xhi) | copy-start | bytes 1081348
  21.6 0.7 copy-start.5
  24.7 9.5 %collective-permute-start.2 = (f32[136,256]{1,0:T(8,128)}, f32[136,256]{1,0:T(8,128)S(1)}, u32[]{:S(2)}, u32[]{:S(2)}) collective-permute-start(f32[136,256]{1,0:T(8,128)} %get-tuple-element.14), channel_id=1, source_target_pairs={{0,1},{1,2},{2,3},{3,4},{4,5},{5,6},{6,7},{7,8},{8,9},{9,10},{10,1... | collective-permute-start | bytes 417800 | tf_op jit(solution)/shard_map/ppermute | solution.py:158
  27.8 8.0 %collective-permute-start.3 = (f32[136,256]{1,0:T(8,128)}, f32[136,256]{1,0:T(8,128)S(1)}, u32[]{:S(2)}, u32[]{:S(2)}) collective-permute-start(f32[136,256]{1,0:T(8,128)} %get-tuple-element.15), channel_id=1, source_target_pairs={{0,15},{1,0},{2,1},{3,2},{4,3},{5,4},{6,5},{7,6},{8,7},{9,8},{10,9... | collective-permute-start | bytes 417800 | tf_op jit(solution)/shard_map/ppermute | solution.py:158
  34.1 1.6 %copy-start.6 = (f32[136,256]{1,0:T(8,128)}, f32[136,256]{1,0:T(8,128)S(1)}, u32[]{:S(2)}) copy-start(f32[136,256]{1,0:T(8,128)S(1)} %collective-permute-done.2.ylo) | copy-start | bytes 417796
  35.7 0.7 copy-start.7
  66.5 22.6 %collective-permute-start.4 = (f32[1,128]{1,0:T(1,128)S(1)}, f32[1,128]{1,0:T(1,128)S(1)}, u32[]{:S(2)}, u32[]{:S(2)}) collective-permute-start(f32[1,128]{1,0:T(1,128)S(1)} %bitcast.9), channel_id=1, source_target_pairs={{0,0},{1,33},{2,66},{3,99},{4,132},{5,165},{6,198},{7,231},{8,264}... | collective-permute-start | bytes 1544 | tf_op jit(solution)/shard_map/ppermute | solution.py:165

commit v2 on v1

--- a/solution.py
+++ b/solution.py
@@ -19,6 +19,7 @@
 Y_BASE = (0, 28, 64, 88, 112)
 Y_ROWS = 136
 PAD = 40
+VMEM_BYTES = 67_043_328
 
 
 def plane_of(field, index, own, low, high):
@@ -28,6 +29,27 @@
     if index >= 8:
         return high.at[base + index - 8]
     return own[field].at[index]
+
+
+def pack_x_kernel(vx, vy, vz, den, ene, first, last, sems):
+    copies = []
+    for n, field in enumerate((vx, vy, vz, den, ene)):
+        width, base = X_WIDTH[n], X_BASE[n]
+        copies.append(pltpu.make_async_copy(field.at[pl.ds(0, width)], first.at[pl.ds(base, width)], sems.at[2 * n]))
+        copies.append(pltpu.make_async_copy(field.at[pl.ds(8 - width, width)], last.at[pl.ds(base, width)], sems.at[2 * n + 1]))
+    for copy in copies:
+        copy.start()
+    for copy in copies:
+        copy.wait()
+
+
+def load_kernel(first, vx, vy, vz, den, ene, *rest):
+    outs, sems = rest[:5], rest[5]
+    copies = [pltpu.make_async_copy(f, o, sems.at[n]) for n, (f, o) in enumerate(zip((vx, vy, vz, den, ene), outs))]
+    for copy in copies:
+        copy.start()
+    for copy in copies:
+        copy.wait()
 
 
 def pack_y_kernel(vx, vy, vz, den, ene, low, high, up, down):
@@ -75,9 +97,11 @@
     ts, vx, vy, vz, den, ene, xlo, xhi, ylo, yhi,
     o_den, o_ene, o_vx, o_vy, o_vz, o_lim,
     s_vx, s_vy, s_vz, s_d, s_e, s_ld, s_me, s_pr, s_nvx, s_sd, s_sm, s_fd, s_fm, s_max,
+    r_den, r_ene, r_vx, r_vy, r_vz, sems,
 ):
     t = ts[0]
     half_t = 0.5 * t
+    outs, results = (o_den, o_ene, o_vx, o_vy, o_vz), (r_den, r_ene, r_vx, r_vy, r_vz)
     own = (vx, vy, vz, den, ene)
     padded = (s_vx, s_vy, s_vz, s_d, s_e)
     for field in range(5):
@@ -140,11 +164,9 @@
         energy = mass / dens
         new_vx = s_nvx[p + 1, 0:32, :]
         speed = jnp.sqrt(0.56 * energy) + jnp.abs(new_vx) + jnp.abs(new_vy) + jnp.abs(new_vz)
-        o_den[p] = dens
-        o_ene[p] = energy
-        o_vx[p] = new_vx
-        o_vy[p] = new_vy
-        o_vz[p] = new_vz
+        for n, (out, result, value) in enumerate(zip(outs, results, (dens, energy, new_vx, new_vy, new_vz))):
+            result[p] = value
+            pltpu.make_async_copy(result.at[p], out.at[p], sems.at[n]).start()
         s_max[...] = jnp.maximum(s_max[...], speed)
         return carry
 
@@ -152,10 +174,16 @@
     fastest = jnp.max(s_max[...], axis=0, keepdims=True)
     fastest = jnp.maximum(fastest[:, :128], fastest[:, 128:])
     o_lim[...] = jnp.broadcast_to(0.5 / fastest, o_lim.shape)
+    for n, (out, result) in enumerate(zip(outs, results)):
+        pltpu.make_async_copy(result, out, sems.at[n]).wait()
 
 
 def shift(x, axes, count, by):
     return lax.ppermute(x, axes, [(i, (i + by) % count) for i in range(count)])
+
+
+def near(x):
+    return pltpu.with_memory_space_constraint(x, pltpu.VMEM)
 
 
 def smallest(spread, sizes):
@@ -174,34 +202,59 @@
     plane = sizes["c"] * sizes["y"] * sizes["x"]
     assert plane == sizes["z"]
     vmem = pl.BlockSpec(memory_space=pltpu.VMEM)
+    hbm = pl.BlockSpec(memory_space=pltpu.HBM)
     tile = jax.ShapeDtypeStruct((8, 32, 256), jnp.float32)
-    lines = jax.ShapeDtypeStruct((Y_ROWS, 256), jnp.float32)
+    lines = pltpu.VMEM((Y_ROWS, 256), jnp.float32)
+    layers = pltpu.VMEM((X_ROWS, 32, 256), jnp.float32)
+    pack_x = pl.pallas_call(
+        pack_x_kernel,
+        out_shape=(layers, layers),
+        in_specs=[hbm] * 5,
+        out_specs=(vmem, vmem),
+        scratch_shapes=[pltpu.SemaphoreType.DMA((10,))],
+        compiler_params=pltpu.CompilerParams(vmem_limit_bytes=VMEM_BYTES - 800_000),
+        name="pack_x",
+    )
+    load = pl.pallas_call(
+        load_kernel,
+        out_shape=(pltpu.VMEM((8, 32, 256), jnp.float32),) * 5,
+        in_specs=[vmem] + [hbm] * 5,
+        out_specs=(vmem,) * 5,
+        scratch_shapes=[pltpu.SemaphoreType.DMA((5,))],
+        compiler_params=pltpu.CompilerParams(vmem_limit_bytes=VMEM_BYTES - 2_900_000),
+        cost_estimate=pl.CostEstimate(flops=0, bytes_accessed=2500000, transcendentals=0),
+        name="load",
+    )
     pack_y = pl.pallas_call(
         pack_y_kernel,
         out_shape=(lines, lines),
         in_specs=[vmem] * 7,
         out_specs=(vmem, vmem),
+        compiler_params=pltpu.CompilerParams(vmem_limit_bytes=2 << 20),
         name="pack_y",
     )
     step = pl.pallas_call(
         step_kernel,
-        out_shape=(tile,) * 5 + (jax.ShapeDtypeStruct((plane, 128), jnp.float32),),
+        out_shape=(tile,) * 5 + (pltpu.VMEM((plane, 128), jnp.float32),),
         in_specs=[pl.BlockSpec(memory_space=pltpu.SMEM)] + [vmem] * 9,
-        out_specs=(vmem,) * 6,
+        out_specs=(hbm,) * 5 + (vmem,),
         scratch_shapes=[pltpu.VMEM((n, PAD, 256), jnp.float32) for n in (14, 12, 12, 12, 12, 12, 12, 12, 10, 10, 10, 9, 9)]
-        + [pltpu.VMEM((32, 256), jnp.float32)],
+        + [pltpu.VMEM((32, 256), jnp.float32)]
+        + [pltpu.VMEM((8, 32, 256), jnp.float32)] * 5
+        + [pltpu.SemaphoreType.DMA((5,))],
+        compiler_params=pltpu.CompilerParams(vmem_limit_bytes=16 << 20),
         name="remap",
     )
 
     def local(density, energy, velocity_x, velocity_y, velocity_z, time_step):
         fields = (velocity_x, velocity_y, velocity_z, density, energy)
-        first = jnp.concatenate([f[:w] for f, w in zip(fields, X_WIDTH)], axis=0)
-        last = jnp.concatenate([f[8 - w :] for f, w in zip(fields, X_WIDTH)], axis=0)
-        xlo = shift(last, GX, gx, 1)
-        xhi = shift(first, GX, gx, -1)
+        first, last = pack_x(*fields)
+        fields = load(first, *fields)
+        xlo = near(shift(last, GX, gx, 1))
+        xhi = near(shift(first, GX, gx, -1))
         up, down = pack_y(*fields, xlo, xhi)
-        ylo = shift(up, GY, gy, 1)
-        yhi = shift(down, GY, gy, -1)
+        ylo = near(shift(up, GY, gy, 1))
+        yhi = near(shift(down, GY, gy, -1))
         *outs, spread = step(time_step, *fields, xlo, xhi, ylo, yhi)
         return (*outs, smallest(spread, sizes))
 

time: 101 us -> 91.4 us (0.905)
  waiting for transfers between devices: 16.5 us -> 8.07 us
  local copies, waits for them, and re-layouts: 3.47 us -> 0.01 us
  starting transfers between devices: 35.4 us -> 38.7 us
    ppermute x4, waiting for transfers between devices: 6.42 us -> 1.35 us  [shift(): return lax.ppermute(x, axes, [(i, (i + by) % count) for i in range(count)])]
    pallas_call x0 -> x2, Pallas kernels: none -> 3.51 us  [the longest x1 2.29 us: local(): fields = load(first, *fields)]
    unnamed x20 -> x2, local copies, waits for them, and re-layouts: 3.45 us -> 0.01 us
    ppermute x1, starting transfers between devices: 12.5 us -> 15.9 us  [smallest(): part = lax.ppermute(part, AXES, pairs)]
    ppermute x1, waiting for transfers between devices: 10.1 us -> 6.71 us  [smallest(): part = lax.ppermute(part, AXES, pairs)]
    pallas_call x1, Pallas kernels: 2.3 us -> 0.12 us  [local(): up, down = pack_y(*fields, xlo, xhi)]
    pallas_call x1, Pallas kernels: 8.14 us -> 6.38 us  [local(): *outs, spread = step(time_step, *fields, xlo, xhi, ylo, yhi)]
  transfers between devices with their start and end apart: 5 -> 5, of which waited for: 5 -> 2; matrix products, arithmetic and copies ran while one was open for 0% -> 0% of each run, Pallas kernels for 0% -> 3%
where the time goes in v2:
time: 91.4 us; the launch traced here: 91.1 us
  starting transfers between devices  38.7 us (42%)
  blocking collectives  32.3 us (35%)
  Pallas kernels  10 us (11%)
  waiting for transfers between devices  8.07 us (9%)
  between operations  1.37 us (1%)
    ppermute x4, starting transfers between devices, shift(): return lax.ppermute(x, axes, [(i, (i + by) % count) for i in range(count)])  22.8 us
    all_to_all x1, blocking collectives, smallest(): lax.all_to_all(spread, PLANE, 0, 0, tiled=True)  21.4 us
    ppermute x1, starting transfers between devices, smallest(): part = lax.ppermute(part, AXES, pairs)  15.9 us
    all_to_all x1, blocking collectives, smallest(): lax.all_to_all(jnp.broadcast_to(part, spread.shape), PLANE, 0, 0, tiled=T...  10.9 us
    ppermute x1, waiting for transfers between devices, smallest(): part = lax.ppermute(part, AXES, pairs)  6.71 us
    pallas_call x1, Pallas kernels, local(): *outs, spread = step(time_step, *fields, xlo, xhi, ylo, yhi)  6.38 us
    pallas_call x1, Pallas kernels, local(): fields = load(first, *fields)  2.29 us
  transfers between devices with their start and end apart: 5, of which 2 were waited for; matrix products, arithmetic and copies ran while one was open for 0% of the time, Pallas kernels for 3%

profile of v2, /device:TPU:1, one launch (start us, length us, event | category | flops | bytes accessed | tf_op | source)
XLA Modules:
  0.0 91.1 jit_solution(11620239005535392726)
XLA Ops:
  0.6 1.2 %pack_x.1 = (f32[11,32,256]{2,1,0:T(8,128)S(1)}, f32[11,32,256]{2,1,0:T(8,128)S(1)}) custom-call(f32[8,32,256]{2,1,0:T(8,128)} %vx.3, f32[8,32,256]{2,1,0:T(8,128)} %vy.3, f32[8,32,256]{2,1,0:T(8,128)} %vz.3, f32[8,32,256]{2,1,0:T(8,128)} %den.3, f32[8,32,256]{2,1,0:T(8,128)} %ene.3), custom_call_target="tpu_custom_call" | custom-call | tf_op jit(solution)/shard_map/pack_x/pallas_call | solution.py:251
  1.9 0.0 copy-start
  1.9 3.0 %collective-permute-start = (f32[11,32,256]{2,1,0:T(8,128)S(1)}, f32[11,32,256]{2,1,0:T(8,128)S(1)}, u32[]{:S(2)}, u32[]{:S(2)}) collective-permute-start(f32[11,32,256]{2,1,0:T(8,128)S(1)} %get-tuple-element.27), channel_id=1, source_target_pairs={{0,16},{16,32},{32,48},{48,64},{64,80},{80,96},{96,112},{112,128},... | collective-permute-start | bytes 1081352 | tf_op jit(solution)/shard_map/ppermute | solution.py:182
  4.9 11.1 %collective-permute-start.1 = (f32[11,32,256]{2,1,0:T(8,128)S(1)}, f32[11,32,256]{2,1,0:T(8,128)S(1)}, u32[]{:S(2)}, u32[]{:S(2)}) collective-permute-start(f32[11,32,256]{2,1,0:T(8,128)S(1)} %get-tuple-element.21.first), channel_id=1, source_target_pairs={{0,1008},{16,0},{32,16},{48,32},{64,48},{80,64},{96,80},{112,96},{... | collective-permute-start | bytes 1081352 | tf_op jit(solution)/shard_map/ppermute | solution.py:182
  16.0 0.0 copy-done
  16.0 2.3 %load.1 = (f32[8,32,256]{2,1,0:T(8,128)S(1)}, f32[8,32,256]{2,1,0:T(8,128)S(1)}, f32[8,32,256]{2,1,0:T(8,128)S(1)}, f32[8,32,256]{2,1,0:T(8,128)S(1)}, f32[8,32,256]{2,1,0:T(8,128)S(1)}) custom-call(f32[11,32,256]{2,1,0:T(8,128)} %copy-done, f32[8,32,256]{2,1,0:T(8,128)} %vx.3, f32[8,32,256]{2,1,0:T(8,128)} %vy.3, f32[8,32,256]{2,1,0:T(8,128)} %vz.3, ...), custom_call_target="tpu_custom_call" | custom-call | bytes 2500000 | tf_op jit(solution)/shard_map/load/pallas_call | solution.py:252
  18.3 0.0 collective-permute-done.low.xlo
  18.3 0.0 collective-permute-done.1.high.xhi
  18.3 0.1 pack_y.1
  18.5 1.9 %collective-permute-start.2 = (f32[136,256]{1,0:T(8,128)S(1)}, f32[136,256]{1,0:T(8,128)S(1)}, u32[]{:S(2)}, u32[]{:S(2)}) collective-permute-start(f32[136,256]{1,0:T(8,128)S(1)} %get-tuple-element.28), channel_id=1, source_target_pairs={{0,1},{1,2},{2,3},{3,4},{4,5},{5,6},{6,7},{7,8},{8,9},{9,10},{10,1... | collective-permute-start | bytes 417800 | tf_op jit(solution)/shard_map/ppermute | solution.py:182
  20.4 6.7 %collective-permute-start.3 = (f32[136,256]{1,0:T(8,128)S(1)}, f32[136,256]{1,0:T(8,128)S(1)}, u32[]{:S(2)}, u32[]{:S(2)}) collective-permute-start(f32[136,256]{1,0:T(8,128)S(1)} %get-tuple-element.29), channel_id=1, source_target_pairs={{0,15},{1,0},{2,1},{3,2},{4,3},{5,4},{6,5},{7,6},{8,7},{9,8},{10,9... | collective-permute-start | bytes 417800 | tf_op jit(solution)/shard_map/ppermute | solution.py:182
  27.7 0.0 collective-permute-done.2.ylo
  27.7 1.3 %collective-permute-done.3.yhi = f32[136,256]{1,0:T(8,128)S(1)} collective-permute-done((f32[136,256]{1,0:T(8,128)S(1)}, f32[136,256]{1,0:T(8,128)S(1)}, u32[]{:S(2)}, u32[]{:S(2)}) %collective-permute-start.3) | collective-permute-done | bytes 139296 | tf_op jit(solution)/shard_map/ppermute | solution.py:182
  29.1 6.4 %remap.1 = (f32[8,32,256]{2,1,0:T(8,128)}, f32[8,32,256]{2,1,0:T(8,128)}, f32[8,32,256]{2,1,0:T(8,128)}, f32[8,32,256]{2,1,0:T(8,128)}, f32[8,32,256]{2,1,0:T(8,128)}, /*index=5*/f32[32,128]{1,0:T(8,128)S(1)}) custom-call(f32[1]{0:T(128)S(6)} %copy.16.ts, f32[8,32,256]{2,1,0:T(8,128)S(1)} %get-tuple-element.22.vx, f32[8,32,256]{2,1,0:T(8,128)S(1)} %get-tuple-element.23.vy, ...), custom_call_target="tpu_custom_call" | custom-call | tf_op jit(solution)/shard_map/remap/pallas_call | solution.py:258
  35.5 21.4 %all_to_all.15 = f32[32,1,128]{2,1,0:T(1,128)S(1)} all-to-all(f32[32,1,128]{2,1,0:T(1,128)S(1)} %bitcast.7), channel_id=1, replica_groups=mesh['z'=32,'c'=2,'y'=4,'x'=4] {'c','y','x'}, dimensions={0} | all-to-all | bytes 32768 | tf_op jit(solution)/shard_map/all_to_all | solution.py:191
  56.9 0.1 reduce_min.18
  56.9 15.9 %collective-permute-start.4 = (f32[1,128]{1,0:T(1,128)S(1)}, f32[1,128]{1,0:T(1,128)S(1)}, u32[]{:S(2)}, u32[]{:S(2)}) collective-permute-start(f32[1,128]{1,0:T(1,128)S(1)} %bitcast.9), channel_id=1, source_target_pairs={{0,0},{1,33},{2,66},{3,99},{4,132},{5,165},{6,198},{7,231},{8,264}... | collective-permute-start | bytes 1544 | tf_op jit(solution)/shard_map/ppermute | solution.py:193
  72.9 6.7 %collective-permute-done.4 = f32[1,128]{1,0:T(1,128)S(1)} collective-permute-done((f32[1,128]{1,0:T(1,128)S(1)}, f32[1,128]{1,0:T(1,128)S(1)}, u32[]{:S(2)}, u32[]{:S(2)}) %collective-permute-start.4) | collective-permute-done | bytes 544 | tf_op jit(solution)/shard_map/ppermute | solution.py:193
  79.6 10.9 %all_to_all.16 = f32[32,1,128]{2,1,0:T(1,128)S(1)} all-to-all(f32[32,1,128]{2,1,0:T(1,128)S(1)} %broadcast_in_dim.9), channel_id=1, replica_groups=mesh['z'=32,'c'=2,'y'=4,'x'=4] {'c','y','x'}, dimensions={0} | all-to-all | bytes 32768 | tf_op jit(solution)/shard_map/all_to_all | solution.py:194
  90.5 0.6 reduce_min.19
  (1 shorter events, 0.0 us)
Async XLA Ops:
  1.9 14.2 %copy-start = (f32[11,32,256]{2,1,0:T(8,128)}, f32[11,32,256]{2,1,0:T(8,128)S(1)}, u32[]{:S(2)}) copy-start(f32[11,32,256]{2,1,0:T(8,128)S(1)} %get-tuple-element.21.first) | copy-start | bytes 1081348
  1.9 16.5 %collective-permute-start = (f32[11,32,256]{2,1,0:T(8,128)S(1)}, f32[11,32,256]{2,1,0:T(8,128)S(1)}, u32[]{:S(2)}, u32[]{:S(2)}) collective-permute-start(f32[11,32,256]{2,1,0:T(8,128)S(1)} %get-tuple-element.27), channel_id=1, source_target_pairs={{0,16},{16,32},{32,48},{48,64},{64,80},{80,96},{96,112},{112,128},... | collective-permute-start | bytes 1081352 | tf_op jit(solution)/shard_map/ppermute | solution.py:182
  4.9 13.4 %collective-permute-start.1 = (f32[11,32,256]{2,1,0:T(8,128)S(1)}, f32[11,32,256]{2,1,0:T(8,128)S(1)}, u32[]{:S(2)}, u32[]{:S(2)}) collective-permute-start(f32[11,32,256]{2,1,0:T(8,128)S(1)} %get-tuple-element.21.first), channel_id=1, source_target_pairs={{0,1008},{16,0},{32,16},{48,32},{64,48},{80,64},{96,80},{112,96},{... | collective-permute-start | bytes 1081352 | tf_op jit(solution)/shard_map/ppermute | solution.py:182
  18.5 9.3 %collective-permute-start.2 = (f32[136,256]{1,0:T(8,128)S(1)}, f32[136,256]{1,0:T(8,128)S(1)}, u32[]{:S(2)}, u32[]{:S(2)}) collective-permute-start(f32[136,256]{1,0:T(8,128)S(1)} %get-tuple-element.28), channel_id=1, source_target_pairs={{0,1},{1,2},{2,3},{3,4},{4,5},{5,6},{6,7},{7,8},{8,9},{9,10},{10,1... | collective-permute-start | bytes 417800 | tf_op jit(solution)/shard_map/ppermute | solution.py:182
  20.4 8.7 %collective-permute-start.3 = (f32[136,256]{1,0:T(8,128)S(1)}, f32[136,256]{1,0:T(8,128)S(1)}, u32[]{:S(2)}, u32[]{:S(2)}) collective-permute-start(f32[136,256]{1,0:T(8,128)S(1)} %get-tuple-element.29), channel_id=1, source_target_pairs={{0,15},{1,0},{2,1},{3,2},{4,3},{5,4},{6,5},{7,6},{8,7},{9,8},{10,9... | collective-permute-start | bytes 417800 | tf_op jit(solution)/shard_map/ppermute | solution.py:182
  56.9 22.6 %collective-permute-start.4 = (f32[1,128]{1,0:T(1,128)S(1)}, f32[1,128]{1,0:T(1,128)S(1)}, u32[]{:S(2)}, u32[]{:S(2)}) collective-permute-start(f32[1,128]{1,0:T(1,128)S(1)} %bitcast.9), channel_id=1, source_target_pairs={{0,0},{1,33},{2,66},{3,99},{4,132},{5,165},{6,198},{7,231},{8,264}... | collective-permute-start | bytes 1544 | tf_op jit(solution)/shard_map/ppermute | solution.py:193

commit v3 on v1

v3 whole, which is shorter than its diff:
```python
import jax
import jax.numpy as jnp
from jax import lax
from jax.experimental import pallas as pl
from jax.experimental.pallas import tpu as pltpu
from jax.sharding import Mesh
from jax.sharding import PartitionSpec as P

AXES = ("z", "c", "y", "x")
GX = ("z", "c")
GY = ("y", "x")
PLANE = ("c", "y", "x")

Y_WIDTH = (2, 3, 2, 2, 2)
Y_BASE = (0, 16, 40, 56, 72)
Y_ROWS = 88
PAD = 40
LAYERS = 7
X_ROWS = LAYERS * 36
VMEM_BYTES = 67_043_328


def above(x, axis):
    return pltpu.roll(x, x.shape[axis] - 1, axis)


def below(x, axis):
    return pltpu.roll(x, 1, axis)


def across(vy, vz):
    return 0.5 * (above(vy, 0) - below(vy, 0)) + 0.5 * (above(vz, 1) - below(vz, 1))


def lagrange(rho, en, move):
    lag_density = rho / (1.0 + move)
    energy_half = en - 0.2 * en * move
    return lag_density, lag_density * (en - 0.4 * energy_half * move)


def van_leer(left, right):
    product = left * right
    agree = product > 0
    return jnp.where(agree, 2.0 * product / jnp.where(agree, left + right, 1.0), 0.0)


def fluxes(half_t, v_here, v_next, here, here_slopes, ahead, ahead_slopes):
    courant = half_t * (v_here + v_next)
    weight = 0.5 * (1.0 - jnp.abs(courant))
    forward = courant > 0
    return [
        courant * jnp.where(forward, f + weight * s, g - weight * r)
        for f, s, g, r in zip(here, here_slopes, ahead, ahead_slopes)
    ]


def sweep_roll(fields, velocity, half_t, axis):
    courant = half_t * (velocity + above(velocity, axis))
    weight = 0.5 * (1.0 - jnp.abs(courant))
    forward = courant > 0
    moved = []
    for field in fields:
        ahead = above(field, axis)
        diff = ahead - field
        slope = van_leer(below(diff, axis), diff)
        flux = courant * jnp.where(forward, field + weight * slope, ahead - weight * above(slope, axis))
        moved.append(field + below(flux, axis) - flux)
    return moved


def finish(fields, new_vx, new_vy, new_vz, half_t):
    fields = [f[:32] for f in sweep_roll(fields, new_vy, half_t, 0)]
    dens, mass = sweep_roll(fields, new_vz, half_t, 1)
    energy = mass / dens
    speed = jnp.sqrt(0.56 * energy) + jnp.abs(new_vx) + jnp.abs(new_vy[:32]) + jnp.abs(new_vz)
    return dens, energy, speed


def load_kernel(*refs):
    fields, outs, (up, down, sems) = refs[:5], refs[5:10], refs[10:]
    copies = [pltpu.make_async_copy(f, o, sems.at[n]) for n, (f, o) in enumerate(zip(fields, outs))]
    for copy in copies:
        copy.start()
    for field, copy in enumerate(copies):
        copy.wait()
        width = Y_WIDTH[field]
        for k in range(8):
            line = Y_BASE[field] + k * width
            up[line : line + width, :] = outs[field][k, 32 - width : 32, :]
            down[line : line + width, :] = outs[field][k, 0:width, :]


def edge_kernel(ts, *refs):
    own, (ylo, yhi), padded, (first, last) = refs[:5], refs[5:7], refs[7:12], refs[12:]
    s_vx, s_vy, s_vz, s_d, s_e = padded
    t = ts[0]

    def pad(field, p):
        width = Y_WIDTH[field]
        line = Y_BASE[field] + p * width
        padded[field][p, 0:32, :] = own[field][p]
        padded[field][p, 32 : 32 + width, :] = yhi[line : line + width, :]
        padded[field][p, PAD - width : PAD, :] = ylo[line : line + width, :]

    for p in range(8):
        for field in range(5):
            pad(field, p)

    for message, edge, inner, sign in ((first, 0, 1, 1), (last, 7, 6, -1)):
        rho, en = s_d[inner], s_e[inner]
        beyond = inner + sign
        diverge = 0.5 * sign * (s_vx[beyond] - s_vx[edge]) + across(s_vy[inner], s_vz[inner])
        lag_density, mass = lagrange(rho, en, t * diverge)
        part = 0.5 * sign * s_vx[inner] + across(s_vy[edge], s_vz[edge])
        layers = (part, s_d[edge], s_e[edge], s_vx[edge], lag_density, mass, 0.4 * rho * en)
        for n, layer in enumerate(layers):
            message[32 * n : 32 * n + 32, :] = layer[:32]
            line = 32 * LAYERS + 4 * n
            message[line : line + 2, :] = layer[32:34]
            message[line + 2 : line + 4, :] = layer[38:40]


def inner_kernel(
    ts, s_vx, s_vy, s_vz, s_d, s_e,
    h_vy, h_vz, o_q, o_ld, o_me, o_nvx, o_nvy, o_nvz, o_sd, o_sm, o_fd, o_fm, o_den, o_ene, o_max,
    s_pr, s_over, sems,
):
    t = ts[0]
    half_t = 0.5 * t
    for p in range(8):
        rho, en = s_d[p], s_e[p]
        pressure = 0.4 * rho * en
        over = half_t / rho
        s_pr[p] = pressure
        s_over[p] = over
        q = across(s_vy[p], s_vz[p])
        if p in (0, 7):
            o_q[p // 7] = q
        else:
            o_ld[p - 1], o_me[p - 1] = lagrange(rho, en, t * (0.5 * (s_vx[p + 1] - s_vx[p - 1]) + q))
        o_nvy[p] = s_vy[p] - over * (above(pressure, 0) - below(pressure, 0))
        pressure, over = pressure[:32], over[:32]
        o_nvz[p] = s_vz[p, 0:32, :] - over * (above(pressure, 1) - below(pressure, 1))
    to_vy = pltpu.make_async_copy(o_nvy.at[:, pl.ds(0, 32)], h_vy, sems.at[0])
    to_vz = pltpu.make_async_copy(o_nvz, h_vz, sems.at[1])
    to_vy.start()
    to_vz.start()
    for p in range(1, 7):
        o_nvx[p - 1] = s_vx[p] - s_over[p] * (s_pr[p + 1] - s_pr[p - 1])
    for p in range(2, 6):
        for field, slope in ((o_ld, o_sd), (o_me, o_sm)):
            slope[p - 2] = van_leer(field[p - 1] - field[p - 2], field[p] - field[p - 1])
    for p in range(2, 5):
        o_fd[p - 2], o_fm[p - 2] = fluxes(
            half_t, o_nvx[p - 1], o_nvx[p],
            (o_ld[p - 1], o_me[p - 1]), (o_sd[p - 2], o_sm[p - 2]), (o_ld[p], o_me[p]), (o_sd[p - 1], o_sm[p - 1]),
        )
    fastest = None
    for p in (3, 4):
        fields = [f[p - 1] + g[p - 3] - g[p - 2] for f, g in ((o_ld, o_fd), (o_me, o_fm))]
        dens, energy, speed = finish(fields, o_nvx[p - 1, 0:32, :], o_nvy[p], o_nvz[p], half_t)
        o_den[p - 3] = dens
        o_ene[p - 3] = energy
        fastest = speed if fastest is None else jnp.maximum(fastest, speed)
    o_max[...] = fastest
    to_vy.wait()
    to_vz.wait()


def outer_kernel(
    ts, xlo, xhi, s_vx, s_d, s_e, i_q, i_ld, i_me, i_nvx, i_nvy, i_nvz, i_sd, i_sm, i_fd, i_fm, i_den, i_ene, i_max,
    h_den, h_ene, h_vx, o_lim,
    s_lo, s_hi, s_ld, s_me, s_nvx, s_sd, s_sm, s_fd, s_fm, r_den, r_ene, sems,
):
    t = ts[0]
    half_t = 0.5 * t
    started = [
        pltpu.make_async_copy(i_den, h_den.at[pl.ds(3, 2)], sems.at[0]),
        pltpu.make_async_copy(i_ene, h_ene.at[pl.ds(3, 2)], sems.at[1]),
        pltpu.make_async_copy(i_nvx.at[:, pl.ds(0, 32)], h_vx.at[pl.ds(1, 6)], sems.at[2]),
    ]
    for copy in started:
        copy.start()

    for message, scratch in ((xlo, s_lo), (xhi, s_hi)):
        for n in range(LAYERS):
            line = 32 * LAYERS + 4 * n
            scratch[n, 0:32, :] = message[32 * n : 32 * n + 32, :]
            scratch[n, 32:34, :] = message[line : line + 2, :]
            scratch[n, 38:40, :] = message[line + 2 : line + 4, :]

    for halo, edge, inner, sign, at_edge, at_halo in ((s_lo, 0, 1, -1, 1, 0), (s_hi, 7, 6, 1, 2, 3)):
        rho, en, vx = s_d[edge], s_e[edge], s_vx[edge]
        rho_h, en_h, vx_h = halo[1], halo[2], halo[3]
        diverge = 0.5 * sign * (vx_h - s_vx[inner]) + i_q[edge // 7]
        s_ld[at_edge], s_me[at_edge] = lagrange(rho, en, t * diverge)
        s_ld[at_halo], s_me[at_halo] = lagrange(rho_h, en_h, t * (halo[0] - 0.5 * sign * vx))
        scale = half_t * sign
        s_nvx[at_edge] = vx - scale * (0.4 * rho_h * en_h - 0.4 * s_d[inner] * s_e[inner]) / rho
        s_nvx[at_halo] = vx_h - scale * (halo[6] - 0.4 * rho * en) / rho_h
    ends = [
        pltpu.make_async_copy(s_nvx.at[n, pl.ds(0, 32)], h_vx.at[p], sems.at[3 + n - 1]) for n, p in ((1, 0), (2, 7))
    ]
    for copy in ends:
        copy.start()

    outer = {-1: 0, 0: 1, 7: 2, 8: 3}

    def state(p, which):
        if p == -2:
            return s_lo[4 + which]
        if p == 9:
            return s_hi[4 + which]
        return (s_ld, s_me)[which][outer[p]] if p in outer else (i_ld, i_me)[which][p - 1]

    def speed_x(p):
        return s_nvx[outer[p]] if p in outer else i_nvx[p - 1]

    slopes_at = {-1: 0, 0: 1, 1: 2, 6: 3, 7: 4, 8: 5}
    for p, n in slopes_at.items():
        for which, slope in ((0, s_sd), (1, s_sm)):
            here = state(p, which)
            slope[n] = van_leer(here - state(p - 1, which), state(p + 1, which) - here)

    def slope_of(p):
        if p in slopes_at:
            return s_sd[slopes_at[p]], s_sm[slopes_at[p]]
        return i_sd[p - 2], i_sm[p - 2]

    faces_at = {-1: 0, 0: 1, 1: 2, 5: 3, 6: 4, 7: 5}
    for p, n in faces_at.items():
        s_fd[n], s_fm[n] = fluxes(
            half_t, speed_x(p), speed_x(p + 1),
            (state(p, 0), state(p, 1)), slope_of(p), (state(p + 1, 0), state(p + 1, 1)), slope_of(p + 1),
        )

    def face(p, which):
        return (s_fd, s_fm)[which][faces_at[p]] if p in faces_at else (i_fd, i_fm)[which][p - 2]

    fastest = i_max[...]
    copies = []
    for n, p in enumerate((0, 1, 2, 5, 6, 7)):
        fields = [state(p, which) + face(p - 1, which) - face(p, which) for which in (0, 1)]
        dens, energy, speed = finish(fields, speed_x(p)[:32], i_nvy[p], i_nvz[p], half_t)
        r_den[n] = dens
        r_ene[n] = energy
        fastest = jnp.maximum(fastest, speed)
        for k, (result, out) in enumerate(((r_den, h_den), (r_ene, h_ene))):
            copies.append(pltpu.make_async_copy(result.at[n], out.at[p], sems.at[5 + 2 * n + k]))
            copies[-1].start()
    fastest = jnp.max(fastest, axis=0, keepdims=True)
    fastest = jnp.maximum(fastest[:, :128], fastest[:, 128:])
    o_lim[...] = jnp.broadcast_to(0.5 / fastest, o_lim.shape)
    for copy in started + ends + copies:
        copy.wait()


def near(x):
    return pltpu.with_memory_space_constraint(x, pltpu.VMEM)


def smallest(spread, sizes):
    nz, count = sizes["z"], spread.shape[0]
    part = jnp.min(lax.all_to_all(spread, PLANE, 0, 0, tiled=True), axis=0, keepdims=True)
    pairs = [(z * count + k, ((z + k) % nz) * count + k) for z in range(nz) for k in range(count)]
    part = lax.ppermute(part, AXES, pairs)
    part = lax.all_to_all(jnp.broadcast_to(part, spread.shape), PLANE, 0, 0, tiled=True)
    return jnp.min(part).reshape(1)


def solution(mesh):
    gx, gy = mesh.devices.shape
    sizes = {"z": gx // 2, "c": 2, "y": 4 if gy == 16 else 1, "x": gy // (4 if gy == 16 else 1)}
    finer = Mesh(mesh.devices.reshape(tuple(sizes[a] for a in AXES)), AXES)
    plane = sizes["c"] * sizes["y"] * sizes["x"]
    assert plane == sizes["z"]
    vmem = pl.BlockSpec(memory_space=pltpu.VMEM)
    hbm = pl.BlockSpec(memory_space=pltpu.HBM)
    smem = pl.BlockSpec(memory_space=pltpu.SMEM)
    tile = jax.ShapeDtypeStruct((8, 32, 256), jnp.float32)

    def kept(*shape):
        return pltpu.VMEM(shape, jnp.float32)

    def padded(n):
        return kept(n, PAD, 256)

    load = pl.pallas_call(
        load_kernel,
        out_shape=(kept(8, 32, 256),) * 5 + (kept(Y_ROWS, 256),) * 2,
        in_specs=[hbm] * 5,
        out_specs=(vmem,) * 7,
        scratch_shapes=[pltpu.SemaphoreType.DMA((5,))],
        compiler_params=pltpu.CompilerParams(vmem_limit_bytes=VMEM_BYTES - 1_700_000),
        name="load",
    )
    edge = pl.pallas_call(
        edge_kernel,
        out_shape=(padded(8),) * 5 + (kept(X_ROWS, 256),) * 2,
        in_specs=[smem] + [vmem] * 7,
        out_specs=(vmem,) * 7,
        compiler_params=pltpu.CompilerParams(vmem_limit_bytes=4 << 20),
        name="edge",
    )
    inner_shapes = (padded(2), padded(6), padded(6), padded(6), padded(8), kept(8, 32, 256)) + (padded(4),) * 2
    inner_shapes += (padded(3),) * 2 + (kept(2, 32, 256),) * 2 + (kept(32, 256),)
    inner = pl.pallas_call(
        inner_kernel,
        out_shape=(tile,) * 2 + inner_shapes,
        in_specs=[smem] + [vmem] * 5,
        out_specs=(hbm,) * 2 + (vmem,) * len(inner_shapes),
        scratch_shapes=[padded(8), padded(8), pltpu.SemaphoreType.DMA((2,))],
        compiler_params=pltpu.CompilerParams(vmem_limit_bytes=8 << 20),
        cost_estimate=pl.CostEstimate(flops=20_000_000, bytes_accessed=2_000_000, transcendentals=0),
        name="inner",
    )
    outer = pl.pallas_call(
        outer_kernel,
        out_shape=(tile,) * 3 + (kept(plane, 128),),
        in_specs=[smem] + [vmem] * (5 + len(inner_shapes)),
        out_specs=(hbm,) * 3 + (vmem,),
        scratch_shapes=[padded(LAYERS)] * 2
        + [padded(4)] * 3
        + [padded(6)] * 4
        + [kept(6, 32, 256)] * 2
        + [pltpu.SemaphoreType.DMA((17,))],
        compiler_params=pltpu.CompilerParams(vmem_limit_bytes=12 << 20),
        name="outer",
    )

    def send(x, axes, count, by):
        return near(lax.ppermute(x, axes, [(i, (i + by) % count) for i in range(count)]))

    def local(density, energy, velocity_x, velocity_y, velocity_z, time_step):
        *fields, up, down = load(velocity_x, velocity_y, velocity_z, density, energy)
        ylo = send(up, GY, gy, 1)
        yhi = send(down, GY, gy, -1)
        *fields, first, last = edge(time_step, *fields, ylo, yhi)
        xlo = send(last, GX, gx, 1)
        xhi = send(first, GX, gx, -1)
        new_vy, new_vz, *inside = inner(time_step, *fields)
        vx, _, _, den, ene = fields
        new_density, new_energy, new_vx, spread = outer(time_step, xlo, xhi, vx, den, ene, *inside)
        return new_density, new_energy, new_vx, new_vy, new_vz, smallest(spread, sizes)

    split = P(GX, GY, None)
    return jax.shard_map(
        local, mesh=finer, in_specs=(split,) * 5 + (P(),), out_specs=(split,) * 5 + (P(),), check_vma=False
    )
```

time: 101 us -> 85.4 us (0.85)
  waiting for transfers between devices: 16.5 us -> 7.42 us
  starting transfers between devices: 35.4 us -> 40 us
  Pallas kernels: 10.4 us -> 5.93 us
  local copies, waits for them, and re-layouts: 3.47 us -> 0.01 us
  blocking collectives: 32.8 us -> 29.8 us
    ppermute x4, waiting for transfers between devices: 6.42 us -> 0.89 us  [send(): lax.ppermute(x, axes, [(i, (i + by) % count) for i in range(count)])]
    pallas_call x2 -> x4, Pallas kernels: 10.4 us -> 5.93 us  [the longest x1 2.43 us: local(): outer(time_step, xlo, xhi, vx, den, ene, *inside)]
    ppermute x1, starting transfers between devices: 12.5 us -> 16.1 us  [smallest(): part = lax.ppermute(part, AXES, pairs)]
    ppermute x1, waiting for transfers between devices: 10.1 us -> 6.53 us  [smallest(): part = lax.ppermute(part, AXES, pairs)]
    unnamed x20 -> x0, local copies, waits for them, and re-layouts: 3.45 us -> none
    all_to_all x1, blocking collectives: 21.9 us -> 18.9 us  [smallest(): lax.all_to_all(spread, PLANE, 0, 0, tiled=True)]
    ppermute x4, starting transfers between devices: 22.9 us -> 23.9 us  [send(): lax.ppermute(x, axes, [(i, (i + by) % count) for i in range(count)])]
  transfers between devices with their start and end apart: 5 -> 5, of which waited for: 5 -> 2; matrix products, arithmetic and copies ran while one was open for 0% -> 0% of each run, Pallas kernels for 0% -> 2%
where the time goes in v3:
time: 85.4 us; the launch traced here: 85.1 us
  starting transfers between devices  40 us (47%)
  blocking collectives  29.8 us (35%)
  waiting for transfers between devices  7.42 us (9%)
  Pallas kernels  5.93 us (7%)
  between operations  1.36 us (2%)
    ppermute x4, starting transfers between devices, send(): lax.ppermute(x, axes, [(i, (i + by) % count) for i in range(count)])  23.9 us
    all_to_all x1, blocking collectives, smallest(): lax.all_to_all(spread, PLANE, 0, 0, tiled=True)  18.9 us
    ppermute x1, starting transfers between devices, smallest(): part = lax.ppermute(part, AXES, pairs)  16.1 us
    all_to_all x1, blocking collectives, smallest(): lax.all_to_all(jnp.broadcast_to(part, spread.shape), PLANE, 0, 0, tiled=T...  10.9 us
    ppermute x1, waiting for transfers between devices, smallest(): part = lax.ppermute(part, AXES, pairs)  6.53 us
    pallas_call x1, Pallas kernels, local(): outer(time_step, xlo, xhi, vx, den, ene, *inside)  2.43 us
    pallas_call x1, Pallas kernels, local(): new_vy, new_vz, *inside = inner(time_step, *fields)  1.91 us
  transfers between devices with their start and end apart: 5, of which 2 were waited for; matrix products, arithmetic and copies ran while one was open for 0% of the time, Pallas kernels for 2%

profile of v3, /device:TPU:1, one launch (start us, length us, event | category | flops | bytes accessed | tf_op | source)
XLA Modules:
  0.0 85.1 jit_solution(11753102254898015398)
XLA Ops:
  0.6 1.3 %load.1 = (f32[8,32,256]{2,1,0:T(8,128)S(1)}, f32[8,32,256]{2,1,0:T(8,128)S(1)}, f32[8,32,256]{2,1,0:T(8,128)S(1)}, f32[8,32,256]{2,1,0:T(8,128)S(1)}, f32[8,32,...) custom-call(f32[8,32,256]{2,1,0:T(8,128)} %refs_0_.1, f32[8,32,256]{2,1,0:T(8,128)} %refs_1_.1, ...), custom_call_target="tpu_custom_call" | custom-call | tf_op jit(solution)/shard_map/load/pallas_call | solution.py:335
  2.0 3.9 %collective-permute-start = (f32[88,256]{1,0:T(8,128)S(1)}, f32[88,256]{1,0:T(8,128)S(1)}, u32[]{:S(2)}, u32[]{:S(2)}) collective-permute-start(f32[88,256]{1,0:T(8,128)S(1)} %get-tuple-element.44), channel_id=1, source_target_pairs={{0,1},{1,2},{2,3},{3,4},{4,5},{5,6},{6,7},{7,8},{8,9},{9,10},{10,1... | collective-permute-start | bytes 270344 | tf_op jit(solution)/shard_map/ppermute | solution.py:332
  5.9 5.6 %collective-permute-start.1 = (f32[88,256]{1,0:T(8,128)S(1)}, f32[88,256]{1,0:T(8,128)S(1)}, u32[]{:S(2)}, u32[]{:S(2)}) collective-permute-start(f32[88,256]{1,0:T(8,128)S(1)} %get-tuple-element.45), channel_id=1, source_target_pairs={{0,15},{1,0},{2,1},{3,2},{4,3},{5,4},{6,5},{7,6},{8,7},{9,8},{10,9... | collective-permute-start | bytes 270344 | tf_op jit(solution)/shard_map/ppermute | solution.py:332
  12.2 0.0 collective-permute-done.refs_5_
  12.2 0.9 %collective-permute-done.1.refs_6_ = f32[88,256]{1,0:T(8,128)S(1)} collective-permute-done((f32[88,256]{1,0:T(8,128)S(1)}, f32[88,256]{1,0:T(8,128)S(1)}, u32[]{:S(2)}, u32[]{:S(2)}) %collective-permute-start.1) | collective-permute-done | bytes 90144 | tf_op jit(solution)/shard_map/ppermute | solution.py:332
  13.1 0.3 edge.1
  13.4 3.2 %collective-permute-start.2 = (f32[252,256]{1,0:T(8,128)S(1)}, f32[252,256]{1,0:T(8,128)S(1)}, u32[]{:S(2)}, u32[]{:S(2)}) collective-permute-start(f32[252,256]{1,0:T(8,128)S(1)} %get-tuple-element.46), channel_id=1, source_target_pairs={{0,16},{16,32},{32,48},{48,64},{64,80},{80,96},{96,112},{112,128},... | collective-permute-start | bytes 774152 | tf_op jit(solution)/shard_map/ppermute | solution.py:332
  16.6 11.1 %collective-permute-start.3 = (f32[252,256]{1,0:T(8,128)S(1)}, f32[252,256]{1,0:T(8,128)S(1)}, u32[]{:S(2)}, u32[]{:S(2)}) collective-permute-start(f32[252,256]{1,0:T(8,128)S(1)} %get-tuple-element.47), channel_id=1, source_target_pairs={{0,1008},{16,0},{32,16},{48,32},{64,48},{80,64},{96,80},{112,96},{... | collective-permute-start | bytes 774152 | tf_op jit(solution)/shard_map/ppermute | solution.py:332
  27.7 1.9 %inner.1 = (f32[8,32,256]{2,1,0:T(8,128)}, f32[8,32,256]{2,1,0:T(8,128)}, f32[2,40,256]{2,1,0:T(8,128)S(1)}, f32[6,40,256]{2,1,0:T(8,128)S(1)}, f32[6,40,256]{2,...) custom-call(f32[1]{0:T(128)S(6)} %copy.16.ts, ...), custom_call_target="tpu_custom_call" | custom-call | flops 20000000 | bytes 2000000 | tf_op jit(solution)/shard_map/inner/pallas_call | solution.py:341
  29.6 0.0 collective-permute-done.2.xlo
  29.6 0.0 collective-permute-done.3.xhi
  29.6 2.4 %outer.1 = (f32[8,32,256]{2,1,0:T(8,128)}, f32[8,32,256]{2,1,0:T(8,128)}, f32[8,32,256]{2,1,0:T(8,128)}, f32[32,128]{1,0:T(8,128)S(1)}) custom-call(f32[1]{0:T(128)S(6)} %copy.16.ts, f32[252,256]{1,0:T(8,128)S(1)} %collective-permute-done.2.xlo, f32[252,256]{1,0:T(8,128)S(1)} %collective-permute-done.3.xhi, f32[8,40,256]{2,1,0:T(8,128)S(1)} %get-tuple-element.48.s_vx, ...), custom_call_target="tpu_custom_call" | custom-call | tf_op jit(solution)/shard_map/outer/pallas_call | solution.py:343
  32.1 18.9 %all_to_all.15 = f32[32,1,128]{2,1,0:T(1,128)S(1)} all-to-all(f32[32,1,128]{2,1,0:T(1,128)S(1)} %bitcast.7), channel_id=1, replica_groups=mesh['z'=32,'c'=2,'y'=4,'x'=4] {'c','y','x'}, dimensions={0} | all-to-all | bytes 32768 | tf_op jit(solution)/shard_map/all_to_all | solution.py:264
  50.9 0.1 reduce_min.18
  51.0 16.1 %collective-permute-start.4 = (f32[1,128]{1,0:T(1,128)S(1)}, f32[1,128]{1,0:T(1,128)S(1)}, u32[]{:S(2)}, u32[]{:S(2)}) collective-permute-start(f32[1,128]{1,0:T(1,128)S(1)} %bitcast.9), channel_id=1, source_target_pairs={{0,0},{1,33},{2,66},{3,99},{4,132},{5,165},{6,198},{7,231},{8,264}... | collective-permute-start | bytes 1544 | tf_op jit(solution)/shard_map/ppermute | solution.py:266
  67.1 6.5 %collective-permute-done.4 = f32[1,128]{1,0:T(1,128)S(1)} collective-permute-done((f32[1,128]{1,0:T(1,128)S(1)}, f32[1,128]{1,0:T(1,128)S(1)}, u32[]{:S(2)}, u32[]{:S(2)}) %collective-permute-start.4) | collective-permute-done | bytes 544 | tf_op jit(solution)/shard_map/ppermute | solution.py:266
  73.6 10.9 %all_to_all.16 = f32[32,1,128]{2,1,0:T(1,128)S(1)} all-to-all(f32[32,1,128]{2,1,0:T(1,128)S(1)} %broadcast_in_dim.9), channel_id=1, replica_groups=mesh['z'=32,'c'=2,'y'=4,'x'=4] {'c','y','x'}, dimensions={0} | all-to-all | bytes 32768 | tf_op jit(solution)/shard_map/all_to_all | solution.py:267
  84.5 0.6 reduce_min.19
  (1 shorter events, 0.0 us)
Async XLA Ops:
  2.0 10.2 %collective-permute-start = (f32[88,256]{1,0:T(8,128)S(1)}, f32[88,256]{1,0:T(8,128)S(1)}, u32[]{:S(2)}, u32[]{:S(2)}) collective-permute-start(f32[88,256]{1,0:T(8,128)S(1)} %get-tuple-element.44), channel_id=1, source_target_pairs={{0,1},{1,2},{2,3},{3,4},{4,5},{5,6},{6,7},{7,8},{8,9},{9,10},{10,1... | collective-permute-start | bytes 270344 | tf_op jit(solution)/shard_map/ppermute | solution.py:332
  5.9 7.2 %collective-permute-start.1 = (f32[88,256]{1,0:T(8,128)S(1)}, f32[88,256]{1,0:T(8,128)S(1)}, u32[]{:S(2)}, u32[]{:S(2)}) collective-permute-start(f32[88,256]{1,0:T(8,128)S(1)} %get-tuple-element.45), channel_id=1, source_target_pairs={{0,15},{1,0},{2,1},{3,2},{4,3},{5,4},{6,5},{7,6},{8,7},{9,8},{10,9... | collective-permute-start | bytes 270344 | tf_op jit(solution)/shard_map/ppermute | solution.py:332
  13.4 16.2 %collective-permute-start.2 = (f32[252,256]{1,0:T(8,128)S(1)}, f32[252,256]{1,0:T(8,128)S(1)}, u32[]{:S(2)}, u32[]{:S(2)}) collective-permute-start(f32[252,256]{1,0:T(8,128)S(1)} %get-tuple-element.46), channel_id=1, source_target_pairs={{0,16},{16,32},{32,48},{48,64},{64,80},{80,96},{96,112},{112,128},... | collective-permute-start | bytes 774152 | tf_op jit(solution)/shard_map/ppermute | solution.py:332
  16.6 13.1 %collective-permute-start.3 = (f32[252,256]{1,0:T(8,128)S(1)}, f32[252,256]{1,0:T(8,128)S(1)}, u32[]{:S(2)}, u32[]{:S(2)}) collective-permute-start(f32[252,256]{1,0:T(8,128)S(1)} %get-tuple-element.47), channel_id=1, source_target_pairs={{0,1008},{16,0},{32,16},{48,32},{64,48},{80,64},{96,80},{112,96},{... | collective-permute-start | bytes 774152 | tf_op jit(solution)/shard_map/ppermute | solution.py:332
  51.0 22.6 %collective-permute-start.4 = (f32[1,128]{1,0:T(1,128)S(1)}, f32[1,128]{1,0:T(1,128)S(1)}, u32[]{:S(2)}, u32[]{:S(2)}) collective-permute-start(f32[1,128]{1,0:T(1,128)S(1)} %bitcast.9), channel_id=1, source_target_pairs={{0,0},{1,33},{2,66},{3,99},{4,132},{5,165},{6,198},{7,231},{8,264}... | collective-permute-start | bytes 1544 | tf_op jit(solution)/shard_map/ppermute | solution.py:266

commit v4 on v3

--- a/solution.py
+++ b/solution.py
@@ -77,7 +77,8 @@
 
 
 def load_kernel(*refs):
-    fields, outs, (up, down, sems) = refs[:5], refs[5:10], refs[10:]
+    fields, outs, (far, close, sems) = refs[:5], refs[5:10], refs[10:]
+    odd = lax.axis_index("x") % 2 == 1
     copies = [pltpu.make_async_copy(f, o, sems.at[n]) for n, (f, o) in enumerate(zip(fields, outs))]
     for copy in copies:
         copy.start()
@@ -86,12 +87,15 @@
         width = Y_WIDTH[field]
         for k in range(8):
             line = Y_BASE[field] + k * width
-            up[line : line + width, :] = outs[field][k, 32 - width : 32, :]
-            down[line : line + width, :] = outs[field][k, 0:width, :]
+            high, low = outs[field][k, 32 - width : 32, :], outs[field][k, 0:width, :]
+            far[line : line + width, :] = jnp.where(odd, high, low)
+            close[line : line + width, :] = jnp.where(odd, low, high)
 
 
 def edge_kernel(ts, *refs):
-    own, (ylo, yhi), padded, (first, last) = refs[:5], refs[5:7], refs[7:12], refs[12:]
+    own, (far, close), padded, messages = refs[:5], refs[5:7], refs[7:12], refs[12:]
+    odd = lax.axis_index("x") % 2 == 1
+    c = lax.axis_index("c")
     s_vx, s_vy, s_vz, s_d, s_e = padded
     t = ts[0]
 
@@ -99,16 +103,18 @@
         width = Y_WIDTH[field]
         line = Y_BASE[field] + p * width
         padded[field][p, 0:32, :] = own[field][p]
-        padded[field][p, 32 : 32 + width, :] = yhi[line : line + width, :]
-        padded[field][p, PAD - width : PAD, :] = ylo[line : line + width, :]
+        a, b = far[line : line + width, :], close[line : line + width, :]
+        padded[field][p, 32 : 32 + width, :] = jnp.where(odd, a, b)
+        padded[field][p, PAD - width : PAD, :] = jnp.where(odd, b, a)
 
     for p in range(8):
         for field in range(5):
             pad(field, p)
 
-    for message, edge, inner, sign in ((first, 0, 1, 1), (last, 7, 6, -1)):
+    for message, side in zip(messages, (c, 1 - c)):
+        edge, inner, beyond = 7 * side, 1 + 5 * side, 2 + 3 * side
+        sign = (1 - 2 * side).astype(jnp.float32)
         rho, en = s_d[inner], s_e[inner]
-        beyond = inner + sign
         diverge = 0.5 * sign * (s_vx[beyond] - s_vx[edge]) + across(s_vy[inner], s_vz[inner])
         lag_density, mass = lagrange(rho, en, t * diverge)
         part = 0.5 * sign * s_vx[inner] + across(s_vy[edge], s_vz[edge])
@@ -168,9 +174,9 @@
 
 
 def outer_kernel(
-    ts, xlo, xhi, s_vx, s_d, s_e, i_q, i_ld, i_me, i_nvx, i_nvy, i_nvz, i_sd, i_sm, i_fd, i_fm, i_den, i_ene, i_max,
+    ts, far, close, s_vx, s_d, s_e, i_q, i_ld, i_me, i_nvx, i_nvy, i_nvz, i_sd, i_sm, i_fd, i_fm, i_den, i_ene, i_max,
     h_den, h_ene, h_vx, o_lim,
-    s_lo, s_hi, s_ld, s_me, s_nvx, s_sd, s_sm, s_fd, s_fm, r_den, r_ene, sems,
+    s_halo, s_ld, s_me, s_nvx, s_sd, s_sm, s_fd, s_fm, r_den, r_ene, sems,
 ):
     t = ts[0]
     half_t = 0.5 * t
@@ -182,12 +188,14 @@
     for copy in started:
         copy.start()
 
-    for message, scratch in ((xlo, s_lo), (xhi, s_hi)):
+    c = lax.axis_index("c")
+    for message, side in ((far, c), (close, 1 - c)):
         for n in range(LAYERS):
             line = 32 * LAYERS + 4 * n
-            scratch[n, 0:32, :] = message[32 * n : 32 * n + 32, :]
-            scratch[n, 32:34, :] = message[line : line + 2, :]
-            scratch[n, 38:40, :] = message[line + 2 : line + 4, :]
+            s_halo[side, n, 0:32, :] = message[32 * n : 32 * n + 32, :]
+            s_halo[side, n, 32:34, :] = message[line : line + 2, :]
+            s_halo[side, n, 38:40, :] = message[line + 2 : line + 4, :]
+    s_lo, s_hi = s_halo.at[0], s_halo.at[1]
 
     for halo, edge, inner, sign, at_edge, at_halo in ((s_lo, 0, 1, -1, 1, 0), (s_hi, 7, 6, 1, 2, 3)):
         rho, en, vx = s_d[edge], s_e[edge], s_vx[edge]
@@ -319,7 +327,7 @@
         out_shape=(tile,) * 3 + (kept(plane, 128),),
         in_specs=[smem] + [vmem] * (5 + len(inner_shapes)),
         out_specs=(hbm,) * 3 + (vmem,),
-        scratch_shapes=[padded(LAYERS)] * 2
+        scratch_shapes=[kept(2, LAYERS, PAD, 256)]
         + [padded(4)] * 3
         + [padded(6)] * 4
         + [kept(6, 32, 256)] * 2
@@ -328,19 +336,18 @@
         name="outer",
     )
 
-    def send(x, axes, count, by):
-        return near(lax.ppermute(x, axes, [(i, (i + by) % count) for i in range(count)]))
+    def exchange(messages, axes, count):
+        far = [(i, (i + (1 if i % 2 else -1)) % count) for i in range(count)]
+        close = [(i, i ^ 1) for i in range(count)]
+        return [near(lax.ppermute(m, axes, pairs)) for m, pairs in zip(messages, (far, close))]
 
     def local(density, energy, velocity_x, velocity_y, velocity_z, time_step):
-        *fields, up, down = load(velocity_x, velocity_y, velocity_z, density, energy)
-        ylo = send(up, GY, gy, 1)
-        yhi = send(down, GY, gy, -1)
-        *fields, first, last = edge(time_step, *fields, ylo, yhi)
-        xlo = send(last, GX, gx, 1)
-        xhi = send(first, GX, gx, -1)
+        *fields, far, close = load(velocity_x, velocity_y, velocity_z, density, energy)
+        *fields, far, close = edge(time_step, *fields, *exchange((far, close), GY, gy))
+        halos = exchange((far, close), GX, gx)
         new_vy, new_vz, *inside = inner(time_step, *fields)
         vx, _, _, den, ene = fields
-        new_density, new_energy, new_vx, spread = outer(time_step, xlo, xhi, vx, den, ene, *inside)
+        new_density, new_energy, new_vx, spread = outer(time_step, *halos, vx, den, ene, *inside)
         return new_density, new_energy, new_vx, new_vy, new_vz, smallest(spread, sizes)
 
     split = P(GX, GY, None)

time: 85.4 us -> 84.8 us (level)
  blocking collectives: 29.8 us -> 20.9 us
  starting transfers between devices: 40 us -> 46.9 us
  waiting for transfers between devices: 7.42 us -> 8.71 us
    all_to_all x1, blocking collectives: 18.9 us -> 9.98 us  [smallest(): lax.all_to_all(spread, PLANE, 0, 0, tiled=True)]
    ppermute x4, starting transfers between devices: 23.9 us -> 30.3 us  [exchange(): lax.ppermute(m, axes, pairs)]
    ppermute x4, waiting for transfers between devices: 0.89 us -> 2.69 us  [exchange(): lax.ppermute(m, axes, pairs)]
where the time goes in v4:
time: 84.8 us; the launch traced here: 84.4 us
  starting transfers between devices  46.9 us (55%)
  blocking collectives  20.9 us (25%)
  waiting for transfers between devices  8.71 us (10%)
  Pallas kernels  5.93 us (7%)
  between operations  1.38 us (2%)
    ppermute x4, starting transfers between devices, exchange(): lax.ppermute(m, axes, pairs)  30.3 us
    ppermute x1, starting transfers between devices, smallest(): part = lax.ppermute(part, AXES, pairs)  16.6 us
    all_to_all x1, blocking collectives, smallest(): lax.all_to_all(jnp.broadcast_to(part, spread.shape), PLANE, 0, 0, tiled=T...  10.9 us
    all_to_all x1, blocking collectives, smallest(): lax.all_to_all(spread, PLANE, 0, 0, tiled=True)  9.98 us
    ppermute x1, waiting for transfers between devices, smallest(): part = lax.ppermute(part, AXES, pairs)  6.02 us
    ppermute x4, waiting for transfers between devices, exchange(): lax.ppermute(m, axes, pairs)  2.69 us
    pallas_call x1, Pallas kernels, local(): outer(time_step, *halos, vx, den, ene, *inside)  2.36 us
    pallas_call x1, Pallas kernels, local(): new_vy, new_vz, *inside = inner(time_step, *fields)  1.92 us
  transfers between devices with their start and end apart: 5, of which 2 were waited for; matrix products, arithmetic and copies ran while one was open for 0% of the time, Pallas kernels for 2%

profile of v4, /device:TPU:1, one launch (start us, length us, event | category | flops | bytes accessed | tf_op | source)
XLA Modules:
  0.0 84.4 jit_solution(17992483243100839354)
XLA Ops:
  0.6 1.3 %load.1 = (f32[8,32,256]{2,1,0:T(8,128)S(1)}, f32[8,32,256]{2,1,0:T(8,128)S(1)}, f32[8,32,256]{2,1,0:T(8,128)S(1)}, f32[8,32,256]{2,1,0:T(8,128)S(1)}, f32[8,32,...) custom-call(f32[8,32,256]{2,1,0:T(8,128)} %refs_0_.1, f32[8,32,256]{2,1,0:T(8,128)} %refs_1_.1, ...), custom_call_target="tpu_custom_call" | custom-call | tf_op jit(solution)/shard_map/load/pallas_call | solution.py:345
  2.0 7.7 %collective-permute-start = (f32[88,256]{1,0:T(8,128)S(1)}, f32[88,256]{1,0:T(8,128)S(1)}, u32[]{:S(2)}, u32[]{:S(2)}) collective-permute-start(f32[88,256]{1,0:T(8,128)S(1)} %get-tuple-element.44), channel_id=1, source_target_pairs={{0,15},{1,2},{2,1},{3,4},{4,3},{5,6},{6,5},{7,8},{8,7},{9,10},{10,... | collective-permute-start | bytes 270344 | tf_op jit(solution)/shard_map/ppermute | solution.py:342
  9.6 1.9 %collective-permute-start.1 = (f32[88,256]{1,0:T(8,128)S(1)}, f32[88,256]{1,0:T(8,128)S(1)}, u32[]{:S(2)}, u32[]{:S(2)}) collective-permute-start(f32[88,256]{1,0:T(8,128)S(1)} %get-tuple-element.45), channel_id=1, source_target_pairs={{0,1},{1,0},{2,3},{3,2},{4,5},{5,4},{6,7},{7,6},{8,9},{9,8},{10,11... | collective-permute-start | bytes 270344 | tf_op jit(solution)/shard_map/ppermute | solution.py:342
  12.2 0.0 collective-permute-done.refs_5_
  12.2 2.7 %collective-permute-done.1.refs_6_ = f32[88,256]{1,0:T(8,128)S(1)} collective-permute-done((f32[88,256]{1,0:T(8,128)S(1)}, f32[88,256]{1,0:T(8,128)S(1)}, u32[]{:S(2)}, u32[]{:S(2)}) %collective-permute-start.1) | collective-permute-done | bytes 90144 | tf_op jit(solution)/shard_map/ppermute | solution.py:342
  14.9 0.3 edge.1
  15.2 5.5 %collective-permute-start.2 = (f32[252,256]{1,0:T(8,128)S(1)}, f32[252,256]{1,0:T(8,128)S(1)}, u32[]{:S(2)}, u32[]{:S(2)}) collective-permute-start(f32[252,256]{1,0:T(8,128)S(1)} %get-tuple-element.46), channel_id=1, source_target_pairs={{0,1008},{16,32},{32,16},{48,64},{64,48},{80,96},{96,80},{112,128}... | collective-permute-start | bytes 774152 | tf_op jit(solution)/shard_map/ppermute | solution.py:342
  20.8 15.2 %collective-permute-start.3 = (f32[252,256]{1,0:T(8,128)S(1)}, f32[252,256]{1,0:T(8,128)S(1)}, u32[]{:S(2)}, u32[]{:S(2)}) collective-permute-start(f32[252,256]{1,0:T(8,128)S(1)} %get-tuple-element.47), channel_id=1, source_target_pairs={{0,16},{16,0},{32,48},{48,32},{64,80},{80,64},{96,112},{112,96},{1... | collective-permute-start | bytes 774152 | tf_op jit(solution)/shard_map/ppermute | solution.py:342
  36.0 1.9 %inner.1 = (f32[8,32,256]{2,1,0:T(8,128)}, f32[8,32,256]{2,1,0:T(8,128)}, f32[2,40,256]{2,1,0:T(8,128)S(1)}, f32[6,40,256]{2,1,0:T(8,128)S(1)}, f32[6,40,256]{2,...) custom-call(f32[1]{0:T(128)S(6)} %copy.16.ts, ...), custom_call_target="tpu_custom_call" | custom-call | flops 20000000 | bytes 2000000 | tf_op jit(solution)/shard_map/inner/pallas_call | solution.py:348
  37.9 0.0 collective-permute-done.2.far
  37.9 0.0 collective-permute-done.3.close
  37.9 2.4 %outer.1 = (f32[8,32,256]{2,1,0:T(8,128)}, f32[8,32,256]{2,1,0:T(8,128)}, f32[8,32,256]{2,1,0:T(8,128)}, f32[32,128]{1,0:T(8,128)S(1)}) custom-call(f32[1]{0:T(128)S(6)} %copy.16.ts, f32[252,256]{1,0:T(8,128)S(1)} %collective-permute-done.2.far, f32[252,256]{1,0:T(8,128)S(1)} %collective-permute-done.3.close, f32[8,40,256]{2,1,0:T(8,128)S(1)} %get-tuple-element.48.s_vx, ...), custom_call_target="tpu_custom_call" | custom-call | tf_op jit(solution)/shard_map/outer/pallas_call | solution.py:350
  40.3 10.0 %all_to_all.15 = f32[32,1,128]{2,1,0:T(1,128)S(1)} all-to-all(f32[32,1,128]{2,1,0:T(1,128)S(1)} %bitcast.7), channel_id=1, replica_groups=mesh['z'=32,'c'=2,'y'=4,'x'=4] {'c','y','x'}, dimensions={0} | all-to-all | bytes 32768 | tf_op jit(solution)/shard_map/all_to_all | solution.py:272
  50.3 0.1 reduce_min.18
  50.3 16.6 %collective-permute-start.4 = (f32[1,128]{1,0:T(1,128)S(1)}, f32[1,128]{1,0:T(1,128)S(1)}, u32[]{:S(2)}, u32[]{:S(2)}) collective-permute-start(f32[1,128]{1,0:T(1,128)S(1)} %bitcast.9), channel_id=1, source_target_pairs={{0,0},{1,33},{2,66},{3,99},{4,132},{5,165},{6,198},{7,231},{8,264}... | collective-permute-start | bytes 1544 | tf_op jit(solution)/shard_map/ppermute | solution.py:274
  66.9 6.0 %collective-permute-done.4 = f32[1,128]{1,0:T(1,128)S(1)} collective-permute-done((f32[1,128]{1,0:T(1,128)S(1)}, f32[1,128]{1,0:T(1,128)S(1)}, u32[]{:S(2)}, u32[]{:S(2)}) %collective-permute-start.4) | collective-permute-done | bytes 544 | tf_op jit(solution)/shard_map/ppermute | solution.py:274
  72.9 10.9 %all_to_all.16 = f32[32,1,128]{2,1,0:T(1,128)S(1)} all-to-all(f32[32,1,128]{2,1,0:T(1,128)S(1)} %broadcast_in_dim.9), channel_id=1, replica_groups=mesh['z'=32,'c'=2,'y'=4,'x'=4] {'c','y','x'}, dimensions={0} | all-to-all | bytes 32768 | tf_op jit(solution)/shard_map/all_to_all | solution.py:275
  83.8 0.6 reduce_min.19
  (1 shorter events, 0.0 us)
Async XLA Ops:
  2.0 10.2 %collective-permute-start = (f32[88,256]{1,0:T(8,128)S(1)}, f32[88,256]{1,0:T(8,128)S(1)}, u32[]{:S(2)}, u32[]{:S(2)}) collective-permute-start(f32[88,256]{1,0:T(8,128)S(1)} %get-tuple-element.44), channel_id=1, source_target_pairs={{0,15},{1,2},{2,1},{3,4},{4,3},{5,6},{6,5},{7,8},{8,7},{9,10},{10,... | collective-permute-start | bytes 270344 | tf_op jit(solution)/shard_map/ppermute | solution.py:342
  9.6 5.3 %collective-permute-start.1 = (f32[88,256]{1,0:T(8,128)S(1)}, f32[88,256]{1,0:T(8,128)S(1)}, u32[]{:S(2)}, u32[]{:S(2)}) collective-permute-start(f32[88,256]{1,0:T(8,128)S(1)} %get-tuple-element.45), channel_id=1, source_target_pairs={{0,1},{1,0},{2,3},{3,2},{4,5},{5,4},{6,7},{7,6},{8,9},{9,8},{10,11... | collective-permute-start | bytes 270344 | tf_op jit(solution)/shard_map/ppermute | solution.py:342
  15.2 22.6 %collective-permute-start.2 = (f32[252,256]{1,0:T(8,128)S(1)}, f32[252,256]{1,0:T(8,128)S(1)}, u32[]{:S(2)}, u32[]{:S(2)}) collective-permute-start(f32[252,256]{1,0:T(8,128)S(1)} %get-tuple-element.46), channel_id=1, source_target_pairs={{0,1008},{16,32},{32,16},{48,64},{64,48},{80,96},{96,80},{112,128}... | collective-permute-start | bytes 774152 | tf_op jit(solution)/shard_map/ppermute | solution.py:342
  20.8 17.1 %collective-permute-start.3 = (f32[252,256]{1,0:T(8,128)S(1)}, f32[252,256]{1,0:T(8,128)S(1)}, u32[]{:S(2)}, u32[]{:S(2)}) collective-permute-start(f32[252,256]{1,0:T(8,128)S(1)} %get-tuple-element.47), channel_id=1, source_target_pairs={{0,16},{16,0},{32,48},{48,32},{64,80},{80,64},{96,112},{112,96},{1... | collective-permute-start | bytes 774152 | tf_op jit(solution)/shard_map/ppermute | solution.py:342
  50.3 22.6 %collective-permute-start.4 = (f32[1,128]{1,0:T(1,128)S(1)}, f32[1,128]{1,0:T(1,128)S(1)}, u32[]{:S(2)}, u32[]{:S(2)}) collective-permute-start(f32[1,128]{1,0:T(1,128)S(1)} %bitcast.9), channel_id=1, source_target_pairs={{0,0},{1,33},{2,66},{3,99},{4,132},{5,165},{6,198},{7,231},{8,264}... | collective-permute-start | bytes 1544 | tf_op jit(solution)/shard_map/ppermute | solution.py:274

commit v5 on v4

--- a/solution.py
+++ b/solution.py
@@ -77,7 +77,7 @@
 
 
 def load_kernel(*refs):
-    fields, outs, (far, close, sems) = refs[:5], refs[5:10], refs[10:]
+    fields, outs, (close, far, sems) = refs[:5], refs[5:10], refs[10:]
     odd = lax.axis_index("x") % 2 == 1
     copies = [pltpu.make_async_copy(f, o, sems.at[n]) for n, (f, o) in enumerate(zip(fields, outs))]
     for copy in copies:
@@ -93,9 +93,8 @@
 
 
 def edge_kernel(ts, *refs):
-    own, (far, close), padded, messages = refs[:5], refs[5:7], refs[7:12], refs[12:]
+    own, (close, far), padded, messages = refs[:5], refs[5:7], refs[7:12], refs[12:]
     odd = lax.axis_index("x") % 2 == 1
-    c = lax.axis_index("c")
     s_vx, s_vy, s_vz, s_d, s_e = padded
     t = ts[0]
 
@@ -111,9 +110,7 @@
         for field in range(5):
             pad(field, p)
 
-    for message, side in zip(messages, (c, 1 - c)):
-        edge, inner, beyond = 7 * side, 1 + 5 * side, 2 + 3 * side
-        sign = (1 - 2 * side).astype(jnp.float32)
+    for message, edge, inner, beyond, sign in zip(messages, (0, 7), (1, 6), (2, 5), (1, -1)):
         rho, en = s_d[inner], s_e[inner]
         diverge = 0.5 * sign * (s_vx[beyond] - s_vx[edge]) + across(s_vy[inner], s_vz[inner])
         lag_density, mass = lagrange(rho, en, t * diverge)
@@ -174,7 +171,7 @@
 
 
 def outer_kernel(
-    ts, far, close, s_vx, s_d, s_e, i_q, i_ld, i_me, i_nvx, i_nvy, i_nvz, i_sd, i_sm, i_fd, i_fm, i_den, i_ene, i_max,
+    ts, xlo, xhi, s_vx, s_d, s_e, i_q, i_ld, i_me, i_nvx, i_nvy, i_nvz, i_sd, i_sm, i_fd, i_fm, i_den, i_ene, i_max,
     h_den, h_ene, h_vx, o_lim,
     s_halo, s_ld, s_me, s_nvx, s_sd, s_sm, s_fd, s_fm, r_den, r_ene, sems,
 ):
@@ -188,8 +185,7 @@
     for copy in started:
         copy.start()
 
-    c = lax.axis_index("c")
-    for message, side in ((far, c), (close, 1 - c)):
+    for message, side in ((xlo, 0), (xhi, 1)):
         for n in range(LAYERS):
             line = 32 * LAYERS + 4 * n
             s_halo[side, n, 0:32, :] = message[32 * n : 32 * n + 32, :]
@@ -336,15 +332,18 @@
         name="outer",
     )
 
-    def exchange(messages, axes, count):
-        far = [(i, (i + (1 if i % 2 else -1)) % count) for i in range(count)]
-        close = [(i, i ^ 1) for i in range(count)]
-        return [near(lax.ppermute(m, axes, pairs)) for m, pairs in zip(messages, (far, close))]
+    def send(x, axes, pairs):
+        return near(lax.ppermute(x, axes, pairs))
+
+    def ring(count, by):
+        return [(i, (i + by) % count) for i in range(count)]
 
     def local(density, energy, velocity_x, velocity_y, velocity_z, time_step):
-        *fields, far, close = load(velocity_x, velocity_y, velocity_z, density, energy)
-        *fields, far, close = edge(time_step, *fields, *exchange((far, close), GY, gy))
-        halos = exchange((far, close), GX, gx)
+        *fields, close, far = load(velocity_x, velocity_y, velocity_z, density, energy)
+        close = send(close, GY, [(i, i ^ 1) for i in range(gy)])
+        far = send(far, GY, [(i, (i + (1 if i % 2 else -1)) % gy) for i in range(gy)])
+        *fields, first, last = edge(time_step, *fields, close, far)
+        halos = send(last, GX, ring(gx, 1)), send(first, GX, ring(gx, -1))
         new_vy, new_vz, *inside = inner(time_step, *fields)
         vx, _, _, den, ene = fields
         new_density, new_energy, new_vx, spread = outer(time_step, *halos, vx, den, ene, *inside)

time: 84.8 us -> 85.3 us (level)
  blocking collectives: 20.9 us -> 29.3 us
  starting transfers between devices: 46.9 us -> 40.3 us
  waiting for transfers between devices: 8.71 us -> 7.53 us
    all_to_all x1, blocking collectives: 9.98 us -> 18.4 us  [smallest(): lax.all_to_all(spread, PLANE, 0, 0, tiled=True)]
    ppermute x4, starting transfers between devices: 30.3 us -> 23.4 us  [send(): return near(lax.ppermute(x, axes, pairs))]
    ppermute x4, waiting for transfers between devices: 2.69 us -> 1.76 us  [send(): return near(lax.ppermute(x, axes, pairs))]
where the time goes in v5:
time: 85.3 us; the launch traced here: 85 us
  starting transfers between devices  40.3 us (47%)
  blocking collectives  29.3 us (34%)
  waiting for transfers between devices  7.53 us (9%)
  Pallas kernels  5.94 us (7%)
  between operations  1.36 us (2%)
    ppermute x4, starting transfers between devices, send(): return near(lax.ppermute(x, axes, pairs))  23.4 us
    all_to_all x1, blocking collectives, smallest(): lax.all_to_all(spread, PLANE, 0, 0, tiled=True)  18.4 us
    ppermute x1, starting transfers between devices, smallest(): part = lax.ppermute(part, AXES, pairs)  16.9 us
    all_to_all x1, blocking collectives, smallest(): lax.all_to_all(jnp.broadcast_to(part, spread.shape), PLANE, 0, 0, tiled=T...  10.9 us
    ppermute x1, waiting for transfers between devices, smallest(): part = lax.ppermute(part, AXES, pairs)  5.77 us
    pallas_call x1, Pallas kernels, local(): outer(time_step, *halos, vx, den, ene, *inside)  2.43 us
    pallas_call x1, Pallas kernels, local(): new_vy, new_vz, *inside = inner(time_step, *fields)  1.91 us
    ppermute x4, waiting for transfers between devices, send(): return near(lax.ppermute(x, axes, pairs))  1.76 us
  transfers between devices with their start and end apart: 5, of which 2 were waited for; matrix products, arithmetic and copies ran while one was open for 0% of the time, Pallas kernels for 2%

profile of v5, /device:TPU:1, one launch (start us, length us, event | category | flops | bytes accessed | tf_op | source)
XLA Modules:
  0.0 85.0 jit_solution(17022135588637172542)
XLA Ops:
  0.6 1.3 %load.1 = (f32[8,32,256]{2,1,0:T(8,128)S(1)}, f32[8,32,256]{2,1,0:T(8,128)S(1)}, f32[8,32,256]{2,1,0:T(8,128)S(1)}, f32[8,32,256]{2,1,0:T(8,128)S(1)}, f32[8,32,...) custom-call(f32[8,32,256]{2,1,0:T(8,128)} %refs_0_.1, f32[8,32,256]{2,1,0:T(8,128)} %refs_1_.1, ...), custom_call_target="tpu_custom_call" | custom-call | tf_op jit(solution)/shard_map/load/pallas_call | solution.py:342
  2.0 3.9 %collective-permute-start = (f32[88,256]{1,0:T(8,128)S(1)}, f32[88,256]{1,0:T(8,128)S(1)}, u32[]{:S(2)}, u32[]{:S(2)}) collective-permute-start(f32[88,256]{1,0:T(8,128)S(1)} %get-tuple-element.44), channel_id=1, source_target_pairs={{0,1},{1,0},{2,3},{3,2},{4,5},{5,4},{6,7},{7,6},{8,9},{9,8},{10,11... | collective-permute-start | bytes 270344 | tf_op jit(solution)/shard_map/ppermute | solution.py:336
  5.9 6.2 %collective-permute-start.1 = (f32[88,256]{1,0:T(8,128)S(1)}, f32[88,256]{1,0:T(8,128)S(1)}, u32[]{:S(2)}, u32[]{:S(2)}) collective-permute-start(f32[88,256]{1,0:T(8,128)S(1)} %get-tuple-element.45), channel_id=1, source_target_pairs={{0,15},{1,2},{2,1},{3,4},{4,3},{5,6},{6,5},{7,8},{8,7},{9,10},{10,... | collective-permute-start | bytes 270344 | tf_op jit(solution)/shard_map/ppermute | solution.py:336
  12.7 0.0 collective-permute-done.refs_5_
  12.8 1.8 %collective-permute-done.1.refs_6_ = f32[88,256]{1,0:T(8,128)S(1)} collective-permute-done((f32[88,256]{1,0:T(8,128)S(1)}, f32[88,256]{1,0:T(8,128)S(1)}, u32[]{:S(2)}, u32[]{:S(2)}) %collective-permute-start.1) | collective-permute-done | bytes 90144 | tf_op jit(solution)/shard_map/ppermute | solution.py:336
  14.5 0.3 edge.1
  14.8 3.6 %collective-permute-start.2 = (f32[252,256]{1,0:T(8,128)S(1)}, f32[252,256]{1,0:T(8,128)S(1)}, u32[]{:S(2)}, u32[]{:S(2)}) collective-permute-start(f32[252,256]{1,0:T(8,128)S(1)} %get-tuple-element.46), channel_id=1, source_target_pairs={{0,16},{16,32},{32,48},{48,64},{64,80},{80,96},{96,112},{112,128},... | collective-permute-start | bytes 774152 | tf_op jit(solution)/shard_map/ppermute | solution.py:336
  18.4 9.6 %collective-permute-start.3 = (f32[252,256]{1,0:T(8,128)S(1)}, f32[252,256]{1,0:T(8,128)S(1)}, u32[]{:S(2)}, u32[]{:S(2)}) collective-permute-start(f32[252,256]{1,0:T(8,128)S(1)} %get-tuple-element.47), channel_id=1, source_target_pairs={{0,1008},{16,0},{32,16},{48,32},{64,48},{80,64},{96,80},{112,96},{... | collective-permute-start | bytes 774152 | tf_op jit(solution)/shard_map/ppermute | solution.py:336
  28.1 1.9 %inner.1 = (f32[8,32,256]{2,1,0:T(8,128)}, f32[8,32,256]{2,1,0:T(8,128)}, f32[2,40,256]{2,1,0:T(8,128)S(1)}, f32[6,40,256]{2,1,0:T(8,128)S(1)}, f32[6,40,256]{2,...) custom-call(f32[1]{0:T(128)S(6)} %copy.16.ts, ...), custom_call_target="tpu_custom_call" | custom-call | flops 20000000 | bytes 2000000 | tf_op jit(solution)/shard_map/inner/pallas_call | solution.py:347
  30.0 0.0 collective-permute-done.2.xlo
  30.0 0.0 collective-permute-done.3.xhi
  30.0 2.4 %outer.1 = (f32[8,32,256]{2,1,0:T(8,128)}, f32[8,32,256]{2,1,0:T(8,128)}, f32[8,32,256]{2,1,0:T(8,128)}, f32[32,128]{1,0:T(8,128)S(1)}) custom-call(f32[1]{0:T(128)S(6)} %copy.16.ts, f32[252,256]{1,0:T(8,128)S(1)} %collective-permute-done.2.xlo, f32[252,256]{1,0:T(8,128)S(1)} %collective-permute-done.3.xhi, f32[8,40,256]{2,1,0:T(8,128)S(1)} %get-tuple-element.48.s_vx, ...), custom_call_target="tpu_custom_call" | custom-call | tf_op jit(solution)/shard_map/outer/pallas_call | solution.py:349
  32.4 18.4 %all_to_all.15 = f32[32,1,128]{2,1,0:T(1,128)S(1)} all-to-all(f32[32,1,128]{2,1,0:T(1,128)S(1)} %bitcast.7), channel_id=1, replica_groups=mesh['z'=32,'c'=2,'y'=4,'x'=4] {'c','y','x'}, dimensions={0} | all-to-all | bytes 32768 | tf_op jit(solution)/shard_map/all_to_all | solution.py:268
  50.8 0.1 reduce_min.18
  50.9 16.9 %collective-permute-start.4 = (f32[1,128]{1,0:T(1,128)S(1)}, f32[1,128]{1,0:T(1,128)S(1)}, u32[]{:S(2)}, u32[]{:S(2)}) collective-permute-start(f32[1,128]{1,0:T(1,128)S(1)} %bitcast.9), channel_id=1, source_target_pairs={{0,0},{1,33},{2,66},{3,99},{4,132},{5,165},{6,198},{7,231},{8,264}... | collective-permute-start | bytes 1544 | tf_op jit(solution)/shard_map/ppermute | solution.py:270
  67.8 5.8 %collective-permute-done.4 = f32[1,128]{1,0:T(1,128)S(1)} collective-permute-done((f32[1,128]{1,0:T(1,128)S(1)}, f32[1,128]{1,0:T(1,128)S(1)}, u32[]{:S(2)}, u32[]{:S(2)}) %collective-permute-start.4) | collective-permute-done | bytes 544 | tf_op jit(solution)/shard_map/ppermute | solution.py:270
  73.5 10.9 %all_to_all.16 = f32[32,1,128]{2,1,0:T(1,128)S(1)} all-to-all(f32[32,1,128]{2,1,0:T(1,128)S(1)} %broadcast_in_dim.9), channel_id=1, replica_groups=mesh['z'=32,'c'=2,'y'=4,'x'=4] {'c','y','x'}, dimensions={0} | all-to-all | bytes 32768 | tf_op jit(solution)/shard_map/all_to_all | solution.py:271
  84.4 0.6 reduce_min.19
  (1 shorter events, 0.0 us)
Async XLA Ops:
  2.0 10.8 %collective-permute-start = (f32[88,256]{1,0:T(8,128)S(1)}, f32[88,256]{1,0:T(8,128)S(1)}, u32[]{:S(2)}, u32[]{:S(2)}) collective-permute-start(f32[88,256]{1,0:T(8,128)S(1)} %get-tuple-element.44), channel_id=1, source_target_pairs={{0,1},{1,0},{2,3},{3,2},{4,5},{5,4},{6,7},{7,6},{8,9},{9,8},{10,11... | collective-permute-start | bytes 270344 | tf_op jit(solution)/shard_map/ppermute | solution.py:336
  5.9 8.6 %collective-permute-start.1 = (f32[88,256]{1,0:T(8,128)S(1)}, f32[88,256]{1,0:T(8,128)S(1)}, u32[]{:S(2)}, u32[]{:S(2)}) collective-permute-start(f32[88,256]{1,0:T(8,128)S(1)} %get-tuple-element.45), channel_id=1, source_target_pairs={{0,15},{1,2},{2,1},{3,4},{4,3},{5,6},{6,5},{7,8},{8,7},{9,10},{10,... | collective-permute-start | bytes 270344 | tf_op jit(solution)/shard_map/ppermute | solution.py:336
  14.8 15.2 %collective-permute-start.2 = (f32[252,256]{1,0:T(8,128)S(1)}, f32[252,256]{1,0:T(8,128)S(1)}, u32[]{:S(2)}, u32[]{:S(2)}) collective-permute-start(f32[252,256]{1,0:T(8,128)S(1)} %get-tuple-element.46), channel_id=1, source_target_pairs={{0,16},{16,32},{32,48},{48,64},{64,80},{80,96},{96,112},{112,128},... | collective-permute-start | bytes 774152 | tf_op jit(solution)/shard_map/ppermute | solution.py:336
  18.4 11.6 %collective-permute-start.3 = (f32[252,256]{1,0:T(8,128)S(1)}, f32[252,256]{1,0:T(8,128)S(1)}, u32[]{:S(2)}, u32[]{:S(2)}) collective-permute-start(f32[252,256]{1,0:T(8,128)S(1)} %get-tuple-element.47), channel_id=1, source_target_pairs={{0,1008},{16,0},{32,16},{48,32},{64,48},{80,64},{96,80},{112,96},{... | collective-permute-start | bytes 774152 | tf_op jit(solution)/shard_map/ppermute | solution.py:336
  50.9 22.6 %collective-permute-start.4 = (f32[1,128]{1,0:T(1,128)S(1)}, f32[1,128]{1,0:T(1,128)S(1)}, u32[]{:S(2)}, u32[]{:S(2)}) collective-permute-start(f32[1,128]{1,0:T(1,128)S(1)} %bitcast.9), channel_id=1, source_target_pairs={{0,0},{1,33},{2,66},{3,99},{4,132},{5,165},{6,198},{7,231},{8,264}... | collective-permute-start | bytes 1544 | tf_op jit(solution)/shard_map/ppermute | solution.py:270

commit v6 on v4

--- a/solution.py
+++ b/solution.py
@@ -270,7 +270,12 @@
 def smallest(spread, sizes):
     nz, count = sizes["z"], spread.shape[0]
     part = jnp.min(lax.all_to_all(spread, PLANE, 0, 0, tiled=True), axis=0, keepdims=True)
-    pairs = [(z * count + k, ((z + k) % nz) * count + k) for z in range(nz) for k in range(count)]
+    ny, nx = sizes["y"], sizes["x"]
+    reach = [max(x, nx - 1 - x) + max(y, ny - 1 - y) for _ in range(sizes["c"]) for y in range(ny) for x in range(nx)]
+    by_reach = sorted(range(count), key=lambda member: reach[member])
+    by_way = sorted(range(nz), key=lambda way: -min(way, nz - way))
+    way_of = dict(zip(by_reach, by_way))
+    pairs = [(z * count + k, ((z + way_of[k]) % nz) * count + k) for z in range(nz) for k in range(count)]
     part = lax.ppermute(part, AXES, pairs)
     part = lax.all_to_all(jnp.broadcast_to(part, spread.shape), PLANE, 0, 0, tiled=True)
     return jnp.min(part).reshape(1)

time: 84.8 us -> 84.5 us (level)
  blocking collectives: 20.9 us -> 36.9 us
  starting transfers between devices: 46.9 us -> 35.8 us
  waiting for transfers between devices: 8.71 us -> 3.39 us
    all_to_all x1, blocking collectives: 10.9 us -> 26.9 us  [smallest(): lax.all_to_all(jnp.broadcast_to(part, spread.shape), PLANE, 0, 0, tiled=T...]
    ppermute x1, starting transfers between devices: 16.6 us -> 5.54 us  [smallest(): part = lax.ppermute(part, AXES, pairs)]
    ppermute x1, waiting for transfers between devices: 6.02 us -> 0.7 us  [smallest(): part = lax.ppermute(part, AXES, pairs)]
where the time goes in v6:
time: 84.5 us; the launch traced here: 84.1 us
  blocking collectives  36.9 us (44%)
  starting transfers between devices  35.8 us (42%)
  Pallas kernels  5.93 us (7%)
  waiting for transfers between devices  3.39 us (4%)
  between operations  1.38 us (2%)
    ppermute x4, starting transfers between devices, exchange(): lax.ppermute(m, axes, pairs)  30.3 us
    all_to_all x1, blocking collectives, smallest(): lax.all_to_all(jnp.broadcast_to(part, spread.shape), PLANE, 0, 0, tiled=T...  26.9 us
    all_to_all x1, blocking collectives, smallest(): lax.all_to_all(spread, PLANE, 0, 0, tiled=True)  9.98 us
    ppermute x1, starting transfers between devices, smallest(): part = lax.ppermute(part, AXES, pairs)  5.54 us
    ppermute x4, waiting for transfers between devices, exchange(): lax.ppermute(m, axes, pairs)  2.69 us
    pallas_call x1, Pallas kernels, local(): outer(time_step, *halos, vx, den, ene, *inside)  2.36 us
    pallas_call x1, Pallas kernels, local(): new_vy, new_vz, *inside = inner(time_step, *fields)  1.92 us
  transfers between devices with their start and end apart: 5, of which 2 were waited for; matrix products, arithmetic and copies ran while one was open for 0% of the time, Pallas kernels for 2%

profile of v6, /device:TPU:1, one launch (start us, length us, event | category | flops | bytes accessed | tf_op | source)
XLA Modules:
  0.0 84.1 jit_solution(18101161876221951762)
XLA Ops:
  0.6 1.3 %load.1 = (f32[8,32,256]{2,1,0:T(8,128)S(1)}, f32[8,32,256]{2,1,0:T(8,128)S(1)}, f32[8,32,256]{2,1,0:T(8,128)S(1)}, f32[8,32,256]{2,1,0:T(8,128)S(1)}, f32[8,32,...) custom-call(f32[8,32,256]{2,1,0:T(8,128)} %refs_0_.1, f32[8,32,256]{2,1,0:T(8,128)} %refs_1_.1, ...), custom_call_target="tpu_custom_call" | custom-call | tf_op jit(solution)/shard_map/load/pallas_call | solution.py:350
  2.0 7.7 %collective-permute-start = (f32[88,256]{1,0:T(8,128)S(1)}, f32[88,256]{1,0:T(8,128)S(1)}, u32[]{:S(2)}, u32[]{:S(2)}) collective-permute-start(f32[88,256]{1,0:T(8,128)S(1)} %get-tuple-element.44), channel_id=1, source_target_pairs={{0,15},{1,2},{2,1},{3,4},{4,3},{5,6},{6,5},{7,8},{8,7},{9,10},{10,... | collective-permute-start | bytes 270344 | tf_op jit(solution)/shard_map/ppermute | solution.py:347
  9.6 1.9 %collective-permute-start.1 = (f32[88,256]{1,0:T(8,128)S(1)}, f32[88,256]{1,0:T(8,128)S(1)}, u32[]{:S(2)}, u32[]{:S(2)}) collective-permute-start(f32[88,256]{1,0:T(8,128)S(1)} %get-tuple-element.45), channel_id=1, source_target_pairs={{0,1},{1,0},{2,3},{3,2},{4,5},{5,4},{6,7},{7,6},{8,9},{9,8},{10,11... | collective-permute-start | bytes 270344 | tf_op jit(solution)/shard_map/ppermute | solution.py:347
  12.2 0.0 collective-permute-done.refs_5_
  12.2 2.7 %collective-permute-done.1.refs_6_ = f32[88,256]{1,0:T(8,128)S(1)} collective-permute-done((f32[88,256]{1,0:T(8,128)S(1)}, f32[88,256]{1,0:T(8,128)S(1)}, u32[]{:S(2)}, u32[]{:S(2)}) %collective-permute-start.1) | collective-permute-done | bytes 90144 | tf_op jit(solution)/shard_map/ppermute | solution.py:347
  14.9 0.3 edge.1
  15.2 5.5 %collective-permute-start.2 = (f32[252,256]{1,0:T(8,128)S(1)}, f32[252,256]{1,0:T(8,128)S(1)}, u32[]{:S(2)}, u32[]{:S(2)}) collective-permute-start(f32[252,256]{1,0:T(8,128)S(1)} %get-tuple-element.46), channel_id=1, source_target_pairs={{0,1008},{16,32},{32,16},{48,64},{64,48},{80,96},{96,80},{112,128}... | collective-permute-start | bytes 774152 | tf_op jit(solution)/shard_map/ppermute | solution.py:347
  20.8 15.2 %collective-permute-start.3 = (f32[252,256]{1,0:T(8,128)S(1)}, f32[252,256]{1,0:T(8,128)S(1)}, u32[]{:S(2)}, u32[]{:S(2)}) collective-permute-start(f32[252,256]{1,0:T(8,128)S(1)} %get-tuple-element.47), channel_id=1, source_target_pairs={{0,16},{16,0},{32,48},{48,32},{64,80},{80,64},{96,112},{112,96},{1... | collective-permute-start | bytes 774152 | tf_op jit(solution)/shard_map/ppermute | solution.py:347
  36.0 1.9 %inner.1 = (f32[8,32,256]{2,1,0:T(8,128)}, f32[8,32,256]{2,1,0:T(8,128)}, f32[2,40,256]{2,1,0:T(8,128)S(1)}, f32[6,40,256]{2,1,0:T(8,128)S(1)}, f32[6,40,256]{2,...) custom-call(f32[1]{0:T(128)S(6)} %copy.16.ts, ...), custom_call_target="tpu_custom_call" | custom-call | flops 20000000 | bytes 2000000 | tf_op jit(solution)/shard_map/inner/pallas_call | solution.py:353
  37.9 0.0 collective-permute-done.2.far
  37.9 0.0 collective-permute-done.3.close
  37.9 2.4 %outer.1 = (f32[8,32,256]{2,1,0:T(8,128)}, f32[8,32,256]{2,1,0:T(8,128)}, f32[8,32,256]{2,1,0:T(8,128)}, f32[32,128]{1,0:T(8,128)S(1)}) custom-call(f32[1]{0:T(128)S(6)} %copy.16.ts, f32[252,256]{1,0:T(8,128)S(1)} %collective-permute-done.2.far, f32[252,256]{1,0:T(8,128)S(1)} %collective-permute-done.3.close, f32[8,40,256]{2,1,0:T(8,128)S(1)} %get-tuple-element.48.s_vx, ...), custom_call_target="tpu_custom_call" | custom-call | tf_op jit(solution)/shard_map/outer/pallas_call | solution.py:355
  40.3 10.0 %all_to_all.15 = f32[32,1,128]{2,1,0:T(1,128)S(1)} all-to-all(f32[32,1,128]{2,1,0:T(1,128)S(1)} %bitcast.7), channel_id=1, replica_groups=mesh['z'=32,'c'=2,'y'=4,'x'=4] {'c','y','x'}, dimensions={0} | all-to-all | bytes 32768 | tf_op jit(solution)/shard_map/all_to_all | solution.py:272
  50.3 0.1 reduce_min.18
  50.3 5.5 %collective-permute-start.4 = (f32[1,128]{1,0:T(1,128)S(1)}, f32[1,128]{1,0:T(1,128)S(1)}, u32[]{:S(2)}, u32[]{:S(2)}) collective-permute-start(f32[1,128]{1,0:T(1,128)S(1)} %bitcast.9), channel_id=1, source_target_pairs={{0,896},{1,641},{2,354},{3,99},{4,676},{5,517},{6,486},{7,327},{8,... | collective-permute-start | bytes 1544 | tf_op jit(solution)/shard_map/ppermute | solution.py:279
  55.8 0.7 collective-permute-done.4
  56.6 26.9 %all_to_all.16 = f32[32,1,128]{2,1,0:T(1,128)S(1)} all-to-all(f32[32,1,128]{2,1,0:T(1,128)S(1)} %broadcast_in_dim.9), channel_id=1, replica_groups=mesh['z'=32,'c'=2,'y'=4,'x'=4] {'c','y','x'}, dimensions={0} | all-to-all | bytes 32768 | tf_op jit(solution)/shard_map/all_to_all | solution.py:280
  83.5 0.6 reduce_min.19
  (1 shorter events, 0.0 us)
Async XLA Ops:
  2.0 10.2 %collective-permute-start = (f32[88,256]{1,0:T(8,128)S(1)}, f32[88,256]{1,0:T(8,128)S(1)}, u32[]{:S(2)}, u32[]{:S(2)}) collective-permute-start(f32[88,256]{1,0:T(8,128)S(1)} %get-tuple-element.44), channel_id=1, source_target_pairs={{0,15},{1,2},{2,1},{3,4},{4,3},{5,6},{6,5},{7,8},{8,7},{9,10},{10,... | collective-permute-start | bytes 270344 | tf_op jit(solution)/shard_map/ppermute | solution.py:347
  9.6 5.3 %collective-permute-start.1 = (f32[88,256]{1,0:T(8,128)S(1)}, f32[88,256]{1,0:T(8,128)S(1)}, u32[]{:S(2)}, u32[]{:S(2)}) collective-permute-start(f32[88,256]{1,0:T(8,128)S(1)} %get-tuple-element.45), channel_id=1, source_target_pairs={{0,1},{1,0},{2,3},{3,2},{4,5},{5,4},{6,7},{7,6},{8,9},{9,8},{10,11... | collective-permute-start | bytes 270344 | tf_op jit(solution)/shard_map/ppermute | solution.py:347
  15.2 22.6 %collective-permute-start.2 = (f32[252,256]{1,0:T(8,128)S(1)}, f32[252,256]{1,0:T(8,128)S(1)}, u32[]{:S(2)}, u32[]{:S(2)}) collective-permute-start(f32[252,256]{1,0:T(8,128)S(1)} %get-tuple-element.46), channel_id=1, source_target_pairs={{0,1008},{16,32},{32,16},{48,64},{64,48},{80,96},{96,80},{112,128}... | collective-permute-start | bytes 774152 | tf_op jit(solution)/shard_map/ppermute | solution.py:347
  20.8 17.1 %collective-permute-start.3 = (f32[252,256]{1,0:T(8,128)S(1)}, f32[252,256]{1,0:T(8,128)S(1)}, u32[]{:S(2)}, u32[]{:S(2)}) collective-permute-start(f32[252,256]{1,0:T(8,128)S(1)} %get-tuple-element.47), channel_id=1, source_target_pairs={{0,16},{16,0},{32,48},{48,32},{64,80},{80,64},{96,112},{112,96},{1... | collective-permute-start | bytes 774152 | tf_op jit(solution)/shard_map/ppermute | solution.py:347
  50.3 6.2 %collective-permute-start.4 = (f32[1,128]{1,0:T(1,128)S(1)}, f32[1,128]{1,0:T(1,128)S(1)}, u32[]{:S(2)}, u32[]{:S(2)}) collective-permute-start(f32[1,128]{1,0:T(1,128)S(1)} %bitcast.9), channel_id=1, source_target_pairs={{0,896},{1,641},{2,354},{3,99},{4,676},{5,517},{6,486},{7,327},{8,... | collective-permute-start | bytes 1544 | tf_op jit(solution)/shard_map/ppermute | solution.py:279
